TPU v7x, 256 devices: a whole 4x4x8 slice. The times are simulated.
256 devices in a mesh: grp: 16 (over y_hi, x, core), tp: 16 (over y_lo, z).
Axes of the slice: x: 4, y: 4 (y_hi: 2, y_lo: 2; y = y_hi * 2 + y_lo), z: 8, core: 2. Of those that a mesh axis runs over, the one named last changes fastest.
Arguments:
- x_rows: bfloat16 [16384, 4096], P(('grp', 'tp')), may hold values from -6 to 6
- norm_gain: float32 [4096], replicated, may hold values from 0.1 to 1.9
- w_query: bfloat16 [4096, 4096], P(None, 'tp'), may hold values from -0.25 to 0.25
- w_keyval: bfloat16 [4096, 2, 1024], P(None, None, 'tp'), may hold values from -0.09375 to 0.09375
- w_out: bfloat16 [4096, 4096], P('tp'), may hold values from -0.75 to 0.75
- prefix_cache: bfloat16 [32, 128, 2, 1024], P('grp', None, None, 'tp'), may hold values from -70 to 70, as said below
- page_table: int32 [32], replicated, may hold values from 0 to 31, each once
- request_ids: int32 [16384], replicated, may hold values from 0 to 31, never falling along the last dimension, each value on 1 to 1024 neighbouring positions
Outputs:
- attn_out: bfloat16 [16384, 4096], P(('grp', 'tp'))
Inputs may be any that keep to these rules, and one draw needn't show every extreme that they name: `request_ids`: request ids never fall along the stream; each of the 32 requests has 1 to 1024 tokens, one exactly 1024. `page_table`: a permutation; physical page f belongs to group f // 2. `prefix_cache`: keys are stored already rotated for their positions.
All inputs are finite; a program needn't handle non-finite values.
Results may differ from a plain program's by a relative error of at most 0.025.
The roundings to bfloat16 on the way count: a program that leaves them out, or rounds other values in their place, can miss the bound.
Values may be sent and summed in bfloat16 or wider, within the bound.
A program may use at most 64 MiB of HBM per device.

v0:
```python
import jax
import jax.numpy as jnp
from jax import lax
from jax.sharding import PartitionSpec as P

KVH = 8
HD = 128
SINKS = 4


def swapped(block, axis, apart):
    count = lax.axis_size(axis)
    route = []
    for low in range(count):
        high = low | 1 << apart
        if high != low and high < count:
            route += [(low, high), (high, low)]
    return lax.ppermute(block, axis, route)


def shifted(block, axis, distance):
    devices = range(lax.axis_size(axis))
    route = [(i - distance, i) for i in devices if i - distance in devices]
    return lax.ppermute(block, axis, route)


def rotate(values, positions):
    half = HD // 2
    freqs = 500000.0 ** (-jnp.arange(half, dtype=jnp.float32) * 2.0 / HD)
    angles = positions.astype(jnp.float32)[:, None] * freqs[None, :]
    cosine = jnp.cos(angles)[:, None, :]
    sine = jnp.sin(angles)[:, None, :]
    first = values[..., :half]
    second = values[..., half:]
    return jnp.concatenate(
        [first * cosine - second * sine, second * cosine + first * sine], axis=-1
    )


def segment_first(request_ids, wanted, count):
    labels = jnp.arange(count, dtype=jnp.int32)
    counts = jnp.sum((request_ids[:, None] == labels[None, :]).astype(jnp.int32), axis=0)
    starts = jnp.cumsum(counts) - counts
    match = wanted[:, None] == labels[None, :]
    return jnp.sum(jnp.where(match, starts[None, :], 0), axis=1)


def join_pair(lower, mine, peer):
    return jnp.where(
        lower, jnp.concatenate([mine, peer], axis=2), jnp.concatenate([peer, mine], axis=2)
    )


def fold_block(state, queries, keys, values, visible):
    run_max, run_sum, run_acc = state
    scores = jnp.einsum(
        "qgrd,kgd->qgrk", queries, keys, preferred_element_type=jnp.float32
    ) * HD ** (-0.5)
    allowed = visible[:, None, None, :]
    scores = jnp.where(allowed, scores, -1e30)
    new_max = jnp.maximum(run_max, jnp.max(scores, axis=-1))
    weights = jnp.where(allowed, jnp.exp(scores - new_max[..., None]), 0.0)
    factor = jnp.exp(run_max - new_max)
    new_sum = run_sum * factor + jnp.sum(weights, axis=-1)
    new_acc = run_acc * factor[..., None] + jnp.einsum(
        "qgrk,kgd->qgrd", weights.astype(jnp.bfloat16), values, preferred_element_type=jnp.float32
    )
    return (new_max, new_sum, new_acc)


def fold_all(
    state, queries, query_pos, query_seg, query_index, keys, values, visible_fn, block_rows
):
    blocks = queries.shape[0] // block_rows

    def in_blocks(array):
        return array.reshape((blocks, block_rows) + array.shape[1:])

    def update_block(item):
        part_state, part_queries, part_pos, part_seg, part_index = item
        return fold_block(
            part_state, part_queries, keys, values, visible_fn(part_pos, part_seg, part_index)
        )

    pieces = (
        tuple((in_blocks(member) for member in state)),
        in_blocks(queries),
        in_blocks(query_pos),
        in_blocks(query_seg),
        in_blocks(query_index),
    )
    result = lax.map(update_block, pieces)
    return tuple((member.reshape((-1,) + member.shape[2:]) for member in result))


def local(x_rows, norm_gain, w_query, w_keyval, w_out, prefix_cache, page_table, request_ids):
    tp_size = lax.axis_size("tp")
    grp_size = lax.axis_size("grp")
    tp_index = lax.axis_index("tp")
    grp_index = lax.axis_index("grp")
    tok_dev = x_rows.shape[0]
    tok_group = tok_dev * tp_size
    heads_dev = w_query.shape[1] // HD
    kv_cols = w_keyval.shape[2]
    kv_need = max(HD, HD * KVH // tp_size)
    kv_heads = kv_need // HD
    per_kv = heads_dev // kv_heads
    pages_dev = prefix_cache.shape[0]
    page_len = prefix_cache.shape[1]
    prefix_len = pages_dev * grp_size * page_len
    seg_count = 2 * grp_size
    block_rows = min(512, tok_group)
    wide = x_rows.astype(jnp.float32)
    variance = jnp.mean(wide * wide, axis=-1, keepdims=True) + 1e-05
    inverse = lax.rsqrt(variance)
    normed = (wide * inverse * norm_gain).astype(jnp.bfloat16)
    kv_weight = w_keyval.reshape(w_keyval.shape[0], 2 * kv_cols)
    piece = lax.all_gather(normed, "tp", axis=0, tiled=True)
    query_part = jnp.dot(piece, w_query, preferred_element_type=jnp.float32)
    kv_part = jnp.dot(piece, kv_weight, preferred_element_type=jnp.float32)
    projected = jnp.concatenate([query_part, kv_part], axis=1)
    query_cols = heads_dev * HD
    group_start = grp_index * tok_group
    token_index = group_start + jnp.arange(tok_group, dtype=jnp.int32)
    own_seg = lax.dynamic_slice_in_dim(request_ids, group_start, tok_group, 0)
    own_pos = prefix_len + token_index - segment_first(request_ids, own_seg, seg_count)
    queries = rotate(projected[:, :query_cols].reshape(tok_group, heads_dev, HD), own_pos).astype(
        jnp.bfloat16
    )
    queries = queries.reshape(tok_group, kv_heads, per_kv, HD)
    kv_local = projected[:, query_cols:].astype(jnp.bfloat16).reshape(tok_group, 2, kv_cols)
    cache_local = prefix_cache.reshape(pages_dev * page_len, 2, kv_cols)
    kv_own = kv_local
    cache_own = cache_local
    kv_peer, cache_peer = swapped((kv_own, cache_own), "tp", 0)
    lower = tp_index >> 0 & 1 == 0
    kv_own = join_pair(lower, kv_own, kv_peer)
    cache_own = join_pair(lower, cache_own, cache_peer)
    keys_own = rotate(
        kv_own[:, 0].reshape(tok_group, kv_heads, HD).astype(jnp.float32), own_pos
    ).astype(jnp.bfloat16)
    values_own = kv_own[:, 1].reshape(tok_group, kv_heads, HD)
    keys_prev, values_prev = shifted((keys_own, values_own), "grp", 1)
    prev_start = jnp.maximum(group_start - tok_group, 0)
    prev_index = group_start - tok_group + jnp.arange(tok_group, dtype=jnp.int32)
    prev_seg = jnp.where(
        grp_index > 0, lax.dynamic_slice_in_dim(request_ids, prev_start, tok_group, 0), -1
    )
    prev_pos = prefix_len + prev_index - segment_first(request_ids, prev_seg, seg_count)
    suffix_keys = jnp.concatenate([keys_prev, keys_own], axis=0)
    suffix_values = jnp.concatenate([values_prev, values_own], axis=0)
    suffix_seg = jnp.concatenate([prev_seg, own_seg], axis=0)
    suffix_pos = jnp.concatenate([prev_pos, own_pos], axis=0)
    suffix_index = jnp.concatenate([prev_index, token_index], axis=0)

    def suffix_visible(query_pos, query_seg, query_index):
        same = (suffix_seg[None, :] == query_seg[:, None]) & (
            suffix_index[None, :] <= query_index[:, None]
        )
        return same & (
            (query_pos[:, None] - suffix_pos[None, :] < prefix_len) | (suffix_pos[None, :] < SINKS)
        )

    start_state = (
        jnp.full((tok_group, kv_heads, per_kv), -1e30, jnp.float32),
        jnp.zeros((tok_group, kv_heads, per_kv), jnp.float32),
        jnp.zeros((tok_group, kv_heads, per_kv, HD), jnp.float32),
    )
    state = fold_all(
        start_state,
        queries,
        own_pos,
        own_seg,
        token_index,
        suffix_keys,
        suffix_values,
        suffix_visible,
        block_rows,
    )
    page_labels = jnp.arange(page_table.shape[0], dtype=jnp.int32)
    cache_keys = cache_own[:, 0].reshape(pages_dev * page_len, kv_heads, HD)
    cache_values = cache_own[:, 1].reshape(pages_dev * page_len, kv_heads, HD)
    piece_keys = lax.all_gather(cache_keys, "grp", axis=0, tiled=True)
    piece_values = lax.all_gather(cache_values, "grp", axis=0, tiled=True)
    rows = piece_keys.shape[0]
    physical = jnp.arange(rows // page_len, dtype=jnp.int32)
    logical = jnp.sum(
        jnp.where(page_table[None, :] == physical[:, None], page_labels[None, :], 0), axis=1
    )
    key_pos = (
        logical[:, None] * page_len + jnp.arange(page_len, dtype=jnp.int32)[None, :]
    ).reshape(rows)

    def prefix_visible(query_pos, query_seg, query_index):
        before = key_pos[None, :] <= query_pos[:, None]
        return before & (
            (query_pos[:, None] - key_pos[None, :] < prefix_len) | (key_pos[None, :] < SINKS)
        )

    state = fold_all(
        state,
        queries,
        own_pos,
        own_seg,
        token_index,
        piece_keys,
        piece_values,
        prefix_visible,
        block_rows,
    )
    attn = (state[2] / state[1][..., None]).reshape(tok_group, heads_dev * HD).astype(jnp.bfloat16)
    rows = attn
    return lax.psum_scatter(
        jnp.dot(rows, w_out, preferred_element_type=jnp.float32).astype(jnp.bfloat16),
        "tp",
        scatter_dimension=0,
        tiled=True,
    )


def solution(mesh):
    placed = (
        P(("grp", "tp"), None),
        P(),
        P(None, "tp"),
        P(None, None, "tp"),
        P("tp", None),
        P("grp", None, None, "tp"),
        P(),
        P(),
    )
    return jax.shard_map(
        local, mesh=mesh, in_specs=placed, out_specs=P(("grp", "tp"), None), check_vma=False
    )
```

profile of v0, /device:TPU:1, one launch (start us, length us, event | category | flops | bytes accessed | tf_op | source)
XLA Modules:
  0.0 373.4 jit_solution(2221443877971759652)
XLA Ops:
  6.5 1.4 fusion.67
  7.9 2.0 fusion.69
  10.1 1.0 copy.36
  11.0 2.6 collective-permute-start.3
  13.6 1.1 convert_reduce_fusion
  14.7 0.1 copy.32
  14.9 0.1 reduce.4
  15.0 0.8 dynamic-slice_select_fusion
  15.9 0.1 collective-permute-done.3
  15.9 0.1 maximum_select_fusion.1
  16.1 0.7 fusion.82
  16.8 0.1 select_reduce_fusion
  17.1 0.8 select_reduce_fusion.2
  17.9 1.0 multiply_cosine_fusion.1
  18.9 96.0 %all-gather.4.cloned.1.call-done = bf16[1024,4096]{1,0:T(8,128)(2,1)} async-done(((bf16[64,4096]{1,0:T(8,128)(2,1)}), bf16[1024,4096]{1,0:T(8,128)(2,1)}) %all-gather.4.cloned.1.call-update) | async-done | bytes 8388624 | tf_op jit(solution)/shard_map/all_gather | solution.py:118
  115.0 6.7 %convolution_convert_fusion.1 = bf16[1024,128]{0,1:T(8,128)(2,1)S(1)} fusion(bf16[1024,4096]{1,0:T(8,128)(2,1)} %all-gather.4.cloned.1.call-done, bf16[4096,128]{0,1:T(8,128)(2,1)} %bitcast.261), kind=kOutput, calls=%fused_computation.79 | convolution fusion | flops 1073872896 | bytes 9699328 | tf_op jit(solution)/shard_map/dot_general | solution.py:120
  121.6 0.1 collective-permute-start
  121.8 2.4 fusion.83
  124.2 4.7 %collective-permute-done = bf16[1024,2,64]{0,2,1:T(8,128)(2,1)S(1)} collective-permute-done((bf16[1024,2,64]{0,2,1:T(8,128)(2,1)S(1)}, bf16[1024,2,64]{0,2,1:T(8,128)(2,1)S(1)}, u32[]{:S(2)}, u32[]{:S(2)}) %collective-permute-start) | collective-permute-done | bytes 262176 | tf_op jit(solution)/shard_map/ppermute | solution.py:18
  128.9 0.1 maximum_select_fusion
  129.1 1.2 fusion.77
  130.3 0.7 pad_maximum_fusion.2
  131.0 4.5 %collective-permute-start.1 = (bf16[1024,1,128]{0,2,1:T(8,128)(2,1)}, bf16[1024,1,128]{0,2,1:T(8,128)(2,1)}, u32[]{:S(2)}, u32[]{:S(2)}) collective-permute-start(bf16[1024,1,128]{0,2,1:T(8,128)(2,1)} %pad_maximum_fusion.2), channel_id=1, source_target_pairs={{0,16},{16,32},{32,48},{48,64},{64,80},{80,96},{96,112},{112,128},... | collective-permute-start | bytes 786440 | tf_op jit(solution)/shard_map/ppermute | solution.py:24
  135.5 0.9 subtract_convert_fusion
  136.4 1.2 concatenate.58
  137.6 0.9 concatenate.57
  138.4 2.1 collective-permute-start.2
  140.6 1.6 pad_maximum_fusion
  142.2 1.1 copy.33
  143.3 1.0 maximum_maximum_fusion
  144.3 1.0 copy.34
  145.3 1.0 pad_maximum_fusion.1
  146.3 0.3 copy.35
  146.6 25.5 %while.27 = (s32[]{:T(128)}, f32[2,512,1,2]{1,3,2,0:T(2,128)S(1)}, f32[2,512,1,2]{1,3,2,0:T(2,128)S(1)}, f32[2,512,1,2,128]{4,1,3,2,0:T(8,128)}, s32[2048]{0:T(1...) while((s32[]{:T(128)}, f32[2,512,1,2]{1,3,2,0:T(2,128)S(1)}, ...), condition=%wide.region_8.9_spmd, body=%wide.region_5.8_spmd.sunk | while | flops 1108483072 | bytes 39688408 | solution.py:92
  146.7 2.1 fusion.106
  148.8 3.2 fusion.107
  152.1 2.9 fusion.108
  155.0 3.4 fusion.110
  158.4 1.0 copy-done.5
  159.4 2.1 fusion.106
  161.6 3.2 fusion.107
  164.8 2.9 fusion.108
  167.7 3.4 fusion.110
  171.1 1.0 copy-done.5
  172.1 45.6 %all-gather.8.cloned.1.call-done = bf16[4096,1,128]{2,0,1:T(8,128)(2,1)} async-done(((bf16[256,1,128]{2,0,1:T(8,128)(2,1)}), bf16[4096,1,128]{2,0,1:T(8,128)(2,1)}) %all-gather.8.cloned.1.call-update) | async-done | bytes 1048592 | tf_op jit(solution)/shard_map/all_gather | solution.py:184
  217.7 41.1 %while.28 = (s32[]{:T(128)}, f32[2,512,1,2]{1,3,2,0:T(2,128)S(1)}, f32[2,512,1,2,128]{4,3,1,0,2:T(2,128)}, f32[2,512,1,2]{1,3,2,0:T(2,128)S(1)}, f32[2,512,1,2]{...) while((s32[]{:T(128)}, f32[2,512,1,2]{1,3,2,0:T(2,128)S(1)}, ...), condition=%wide.region_13.14_spmd.clone, body=%wide.region_10.13_spmd.clone.sunk | while | flops 2212773888 | bytes 71670216 | solution.py:92
  217.7 0.1 add_bitcast_fusion.2
  217.8 0.1 broadcast_compare_fusion.5
  217.9 2.6 fusion.113
  220.5 5.1 %fusion.114 = (f32[512,2]{0,1:T(2,128)S(1)}, f32[512,2,4096]{2,0,1:T(8,128)S(1)}) fusion(pred[512,4096]{1,0:T(8,128)(4,1)S(1)} %fusion.113, bf16[4096,1,128]{2,0,1:T(8,128)(2,1)} %get-tuple-element.555, bf16[2,512,1,2,128]{4,1,3,2,0:T(8,128)(2,1)} %get-tuple-element.554, s32[]{:T(128)S(6)} %copy.72), kind=kOutput, calls=%fused_computation.39.clone.1 | convolution fusion | flops 1086323712 | bytes 20189188 | tf_op jit(solution)/shard_map/while/body/eval_jaxpr/qgrd,kgd->qgrk/dot_general | solution.py:56
  225.7 5.3 %fusion.116 = f32[512,2]{0,1:T(2,128)S(1)} fusion(f32[512,2,4096]{2,0,1:T(8,128)S(1)} %get-tuple-element.478, f32[512,2]{0,1:T(2,128)S(1)} %get-tuple-element.480, pred[512,4096]{1,0:T(8,128)(4,1)S(1)} %fusion.113), kind=kLoop, calls=%fused_computation.41.clone.1 | loop fusion | flops 20970496 | bytes 18882560 | tf_op jit(solution)/shard_map/while/body/eval_jaxpr/reduce_sum | solution.py:64
  231.0 6.0 %fusion.118 = f32[1,512,1,2,128]{4,1,3,2,0:T(8,128)S(1)} fusion(f32[512,2,4096]{2,0,1:T(8,128)S(1)} %get-tuple-element.478, f32[512,2]{0,1:T(2,128)S(1)} %get-tuple-element.480, pred[512,4096]{1,0:T(8,128)(4,1)S(1)} %fusion.113, bf16[4096,1,128]{2,0,1:T(8,128)(2,1)S(1)} %copy-done.3, f32[2,512,1,2,128]{4,1,3,2,0:T(8,128)S(1)} %copy-done.6, ...), kind=kOutput, calls=%fused_computation.50.clone.1 | convolution fusion | flops 1094975488 | bytes 20979716 | tf_op jit(solution)/shard_map/while/body/eval_jaxpr/qgrk,kgd->qgrd/dot_general | solution.py:65
  237.0 1.2 copy_dynamic-update-slice_fusion.2
  238.2 0.1 add_bitcast_fusion.2
  238.3 0.1 broadcast_compare_fusion.5
  238.4 2.6 fusion.113
  241.0 5.1 %fusion.114 = (f32[512,2]{0,1:T(2,128)S(1)}, f32[512,2,4096]{2,0,1:T(8,128)S(1)}) fusion(pred[512,4096]{1,0:T(8,128)(4,1)S(1)} %fusion.113, bf16[4096,1,128]{2,0,1:T(8,128)(2,1)} %get-tuple-element.555, bf16[2,512,1,2,128]{4,1,3,2,0:T(8,128)(2,1)} %get-tuple-element.554, s32[]{:T(128)S(6)} %copy.72), kind=kOutput, calls=%fused_computation.39.clone.1 | convolution fusion | flops 1086323712 | bytes 20189188 | tf_op jit(solution)/shard_map/while/body/eval_jaxpr/qgrd,kgd->qgrk/dot_general | solution.py:56
  246.2 5.3 %fusion.116 = f32[512,2]{0,1:T(2,128)S(1)} fusion(f32[512,2,4096]{2,0,1:T(8,128)S(1)} %get-tuple-element.478, f32[512,2]{0,1:T(2,128)S(1)} %get-tuple-element.480, pred[512,4096]{1,0:T(8,128)(4,1)S(1)} %fusion.113), kind=kLoop, calls=%fused_computation.41.clone.1 | loop fusion | flops 20970496 | bytes 18882560 | tf_op jit(solution)/shard_map/while/body/eval_jaxpr/reduce_sum | solution.py:64
  251.5 6.0 %fusion.118 = f32[1,512,1,2,128]{4,1,3,2,0:T(8,128)S(1)} fusion(f32[512,2,4096]{2,0,1:T(8,128)S(1)} %get-tuple-element.478, f32[512,2]{0,1:T(2,128)S(1)} %get-tuple-element.480, pred[512,4096]{1,0:T(8,128)(4,1)S(1)} %fusion.113, bf16[4096,1,128]{2,0,1:T(8,128)(2,1)S(1)} %copy-done.3, f32[2,512,1,2,128]{4,1,3,2,0:T(8,128)S(1)} %copy-done.6, ...), kind=kOutput, calls=%fused_computation.50.clone.1 | convolution fusion | flops 1094975488 | bytes 20979716 | tf_op jit(solution)/shard_map/while/body/eval_jaxpr/qgrk,kgd->qgrd/dot_general | solution.py:65
  257.6 1.2 copy_dynamic-update-slice_fusion.2
  258.8 0.2 copy.39
  259.0 1.2 div.34
  260.2 6.8 %convolution_convert_fusion = bf16[1024,4096]{1,0:T(8,128)(2,1)} fusion(bf16[256,4096]{1,0:T(8,128)(2,1)S(1)} %copy-done, f32[128,8,2,128]{3,2,1,0:T(2,128)S(1)} %bitcast.248, f32[128,8,2,128]{3,2,1,0:T(2,128)} %bitcast.249), kind=kOutput, calls=%fused_computation.74 | convolution fusion | flops 2152202240 | bytes 12582912 | tf_op jit(solution)/shard_map/dot_general | solution.py:214
  267.1 99.8 %reduce-scatter.2.cloned.1.call-done = bf16[64,4096]{1,0:T(8,128)(2,1)} async-done(((bf16[1024,4096]{1,0:T(8,128)(2,1)}), bf16[64,4096]{1,0:T(8,128)(2,1)}) %reduce-scatter.2.cloned.1.call-update) | async-done | bytes 524304 | tf_op jit(solution)/shard_map/reduce_scatter | solution.py:213
  (68 shorter events, 0.7 us)
Async XLA Ops:
  6.5 253.7 %copy-start = (bf16[256,4096]{1,0:T(8,128)(2,1)S(1)}, bf16[256,4096]{1,0:T(8,128)(2,1)}, u32[]{:S(2)}) copy-start(bf16[256,4096]{1,0:T(8,128)(2,1)} %param.16) | copy-start | bytes 6291460
  6.5 108.4 %all-gather.4.cloned.1.call-start = ((), (), s32[]{:S(2)}) async-start(), calls=%async_computation.1 | async-start | bytes 8912896 | tf_op jit(solution)/shard_map/all_gather | solution.py:118
  10.0 162.1 %all-gather.6.cloned.1.call-start = ((), (), s32[]{:S(2)}) async-start(), calls=%async_computation.2 | async-start | bytes 1114112 | tf_op jit(solution)/shard_map/all_gather | solution.py:183
  11.0 4.9 %collective-permute-start.3 = (bf16[256,2,64]{2,0,1:T(8,128)(2,1)S(1)}, bf16[256,2,64]{2,0,1:T(8,128)(2,1)S(1)}, u32[]{:S(2)}, u32[]{:S(2)}) collective-permute-start(bf16[256,2,64]{2,0,1:T(8,128)(2,1)S(1)} %bitcast.251), channel_id=1, source_target_pairs={{0,1},{1,0},{2,3},{3,2},{4,5},{5,4},{6,7},{7,6},{8,9},{9,8},{10,11... | collective-permute-start | bytes 196616 | tf_op jit(solution)/shard_map/ppermute | solution.py:18
  16.8 200.9 %all-gather.8.cloned.1.call-start = ((), (), s32[]{:S(2)}) async-start(), calls=%async_computation.3 | async-start | bytes 1114112 | tf_op jit(solution)/shard_map/all_gather | solution.py:184
  18.9 348.0 %reduce-scatter.2.cloned.1.call-start = ((), (), s32[]{:S(2)}) async-start(), calls=%async_computation.4 | async-start | bytes 8912896 | tf_op jit(solution)/shard_map/reduce_scatter | solution.py:213
  115.0 6.8 %copy-start.1 = (bf16[1024,4096]{1,0:T(8,128)(2,1)S(1)}, bf16[1024,4096]{1,0:T(8,128)(2,1)}, u32[]{:S(2)}) copy-start(bf16[1024,4096]{1,0:T(8,128)(2,1)} %all-gather.4.cloned.1.call-done) | copy-start | bytes 25165828
  115.0 6.8 %copy-start.2 = (bf16[4096,256]{1,0:T(8,128)(2,1)S(1)}, bf16[4096,256]{1,0:T(8,128)(2,1)}, u32[]{:S(2)}) copy-start(bf16[4096,256]{1,0:T(8,128)(2,1)} %param.14) | copy-start | bytes 6291460
  121.6 7.3 %collective-permute-start = (bf16[1024,2,64]{0,2,1:T(8,128)(2,1)S(1)}, bf16[1024,2,64]{0,2,1:T(8,128)(2,1)S(1)}, u32[]{:S(2)}, u32[]{:S(2)}) collective-permute-start(bf16[1024,2,64]{0,2,1:T(8,128)(2,1)S(1)} %bitcast.253), channel_id=1, source_target_pairs={{0,1},{1,0},{2,3},{3,2},{4,5},{5,4},{6,7},{7,6},{8,9},{9,8},{10,11... | collective-permute-start | bytes 786440 | tf_op jit(solution)/shard_map/ppermute | solution.py:18
  131.0 12.3 %collective-permute-start.1 = (bf16[1024,1,128]{0,2,1:T(8,128)(2,1)}, bf16[1024,1,128]{0,2,1:T(8,128)(2,1)}, u32[]{:S(2)}, u32[]{:S(2)}) collective-permute-start(bf16[1024,1,128]{0,2,1:T(8,128)(2,1)} %pad_maximum_fusion.2), channel_id=1, source_target_pairs={{0,16},{16,32},{32,48},{48,64},{64,80},{80,96},{96,112},{112,128},... | collective-permute-start | bytes 786440 | tf_op jit(solution)/shard_map/ppermute | solution.py:24
  138.4 6.9 %collective-permute-start.2 = (bf16[1024,1,128]{0,2,1:T(8,128)(2,1)S(1)}, bf16[1024,1,128]{0,2,1:T(8,128)(2,1)}, u32[]{:S(2)}, u32[]{:S(2)}) collective-permute-start(bf16[1024,1,128]{0,2,1:T(8,128)(2,1)S(1)} %get-tuple-element.302), channel_id=1, source_target_pairs={{0,16},{16,32},{32,48},{48,64},{64,80},{80,96},{96,112},{112,128},... | collective-permute-start | bytes 786440 | tf_op jit(solution)/shard_map/ppermute | solution.py:24
  148.8 6.2 %copy-start.4 = (f32[2,512,1,2,128]{4,1,3,2,0:T(8,128)S(1)}, f32[2,512,1,2,128]{4,1,3,2,0:T(8,128)}, u32[]{:S(2)}) copy-start(f32[2,512,1,2,128]{4,1,3,2,0:T(8,128)} %get-tuple-element.499) | copy-start | bytes 3145732 | tf_op jit(solution)/shard_map/while
  158.4 1.0 copy-start.5
  161.6 6.2 %copy-start.4 = (f32[2,512,1,2,128]{4,1,3,2,0:T(8,128)S(1)}, f32[2,512,1,2,128]{4,1,3,2,0:T(8,128)}, u32[]{:S(2)}) copy-start(f32[2,512,1,2,128]{4,1,3,2,0:T(8,128)} %get-tuple-element.499) | copy-start | bytes 3145732 | tf_op jit(solution)/shard_map/while
  171.1 1.0 copy-start.5
  225.7 5.3 %copy-start.3 = (bf16[4096,1,128]{2,0,1:T(8,128)(2,1)S(1)}, bf16[4096,1,128]{2,0,1:T(8,128)(2,1)}, u32[]{:S(2)}) copy-start(bf16[4096,1,128]{2,0,1:T(8,128)(2,1)} %get-tuple-element.557) | copy-start | bytes 3145732 | tf_op jit(solution)/shard_map/while
  225.7 5.3 %copy-start.6 = (f32[2,512,1,2,128]{4,1,3,2,0:T(8,128)S(1)}, f32[2,512,1,2,128]{4,1,3,2,0:T(8,128)}, u32[]{:S(2)}) copy-start(f32[2,512,1,2,128]{4,1,3,2,0:T(8,128)} %get-tuple-element.556) | copy-start | bytes 3145732 | tf_op jit(solution)/shard_map/while
  246.2 5.3 %copy-start.3 = (bf16[4096,1,128]{2,0,1:T(8,128)(2,1)S(1)}, bf16[4096,1,128]{2,0,1:T(8,128)(2,1)}, u32[]{:S(2)}) copy-start(bf16[4096,1,128]{2,0,1:T(8,128)(2,1)} %get-tuple-element.557) | copy-start | bytes 3145732 | tf_op jit(solution)/shard_map/while
  246.2 5.3 %copy-start.6 = (f32[2,512,1,2,128]{4,1,3,2,0:T(8,128)S(1)}, f32[2,512,1,2,128]{4,1,3,2,0:T(8,128)}, u32[]{:S(2)}) copy-start(f32[2,512,1,2,128]{4,1,3,2,0:T(8,128)} %get-tuple-element.556) | copy-start | bytes 3145732 | tf_op jit(solution)/shard_map/while
Sparse Core Ops, SparseCore 0:
  10.1 104.8 all-gather.3
  117.7 48.2 all-gather.5
  168.7 48.9 all-gather.7
  267.2 99.6 reduce-scatter.1
where the time goes:
time: 374 us; the launch traced here: 373 us
  waiting for transfers between devices  246 us (66%)
  matrix products  51.4 us (14%)
  other arithmetic  40.5 us (11%)
  between operations  13.4 us (4%)
  local copies, waits for them, and re-layouts  12.1 us (3%)
  starting transfers between devices  9.4 us (3%)
    reduce_scatter x1, waiting for transfers between devices, local(): lax.psum_scatter(jnp.dot(rows, w_out, preferred_element_type=jnp.float32)...  99.8 us
    all_gather x1, waiting for transfers between devices, local(): piece = lax.all_gather(normed, 'tp', axis=0, tiled=True)  96 us
    all_gather x1, waiting for transfers between devices, local(): piece_values = lax.all_gather(cache_values, 'grp', axis=0, tiled=True)  45.6 us
    dot_general x4, matrix products, fold_block(): jnp.einsum('qgrk,kgd->qgrd', weights.astype(jnp.bfloat16), values, prefer...  18.8 us
    dot_general x4, matrix products, fold_block(): jnp.einsum('qgrd,kgd->qgrk', queries, keys, preferred_element_type=jnp.fl...  16.7 us
    reduce_sum x4, other arithmetic, fold_block(): new_sum = run_sum * factor + jnp.sum(weights, axis=-1)  16.3 us
  transfers between devices with their start and end apart: 8, of which 5 were waited for; matrix products, arithmetic and copies ran while one was open for 13% of the time, Pallas kernels for 0%

commit v1 on v0

v1 whole, which is shorter than its diff:
```python
import math

import jax
import jax.numpy as jnp
from jax import lax
from jax.experimental import pallas as pl
from jax.experimental.pallas import tpu as pltpu
from jax.sharding import PartitionSpec as P

MESH = pl.DeviceIdType.MESH
HD = 128
SINKS = 4
D = 4096
CH = 64
NZ = 8
HALF = CH * NZ
PREFIX = 4096
SCALE = HD**-0.5 * math.log2(math.e)
NEG = -1e30
BF = jnp.bfloat16
F32 = jnp.float32

RING, PZ, PY, PX, PSIB, WY, WSIB, KVZ, KVH, RS = 0, 16, 17, 20, 23, 24, 27, 30, 38, 40
MESSAGES = 56


def ring_id(base, d, h, p):
    return base + (d * 4 + (h - 1)) * 2 + p


def kernel(
    x_ref,
    gain_ref,
    pre_ref,
    kpe_ref,
    off_ref,
    cos_ref,
    sin_ref,
    wq_ref,
    wkv_ref,
    wo_ref,
    out_ref,
    xall,
    wq,
    wkv,
    wo,
    px,
    kvs,
    qpad,
    st_m,
    st_l,
    st_acc,
    attn,
    sbuf,
    rbuf,
    ssem,
    rsem,
    lsem,
):
    g = lax.axis_index("grp")
    t = lax.axis_index("tp")
    core = g % 2
    xx = (g // 2) % 4
    hi = g // 8
    z = t % NZ
    lo = t // NZ
    par = z % 2
    up = (g, lo * NZ + (z + 1) % NZ)
    down = (g, lo * NZ + (z + NZ - 1) % NZ)
    pair = (g, t + 1 - 2 * par)
    other_t = (1 - lo) * NZ + z
    other_g = (1 - hi) * 8 + xx * 2 + core
    sibling = (g + 1 - 2 * core, t)
    weight_peer = (core * other_g + (1 - core) * g, other_t)

    def along_x(k):
        return (hi * 8 + ((xx + k) % 4) * 2 + core, t)

    def half_group(k):
        index = (2 * g + lo + k + 32) % 32
        return (index // 2, (index % 2) * NZ + z)

    def remote(src, dst, number, device):
        return pltpu.make_async_remote_copy(
            src_ref=src,
            dst_ref=dst,
            send_sem=ssem.at[number],
            recv_sem=rsem.at[number],
            device_id=device,
            device_id_type=MESH,
        )

    def arrived(ref, number):
        remote(ref, ref, number, sibling).wait_recv()

    def left(ref, number):
        remote(ref, ref, number, sibling).wait_send()

    ahead = (up, down)
    sign = (1, -1)

    def rows_of(p):
        return pl.ds(p * 32, 32)

    def origin(d, h):
        return (z - sign[d] * h + NZ) % NZ

    local_wq = pltpu.make_async_copy(wq_ref, wq.at[lo], lsem.at[0])
    local_wkv = pltpu.make_async_copy(wkv_ref, wkv.at[lo], lsem.at[1])
    local_wo = pltpu.make_async_copy(wo_ref, wo.at[lo], lsem.at[2])
    local_wq.start()
    local_wkv.start()
    local_wo.start()
    wide = x_ref[...].astype(F32)
    variance = jnp.mean(wide * wide, axis=-1, keepdims=True) + 1e-05
    xall[z] = (wide * lax.rsqrt(variance) * gain_ref[...]).astype(BF)
    px[lo, hi, xx, core, par] = pre_ref[...]
    for d in range(2):
        rbuf[d, 3, rows_of(1 - d)] = jnp.zeros((32, D), BF)

    partners = [up, down, (g, other_t), (other_g, other_t), (other_g, t)]
    partners += [along_x(1), along_x(2), along_x(3), sibling]
    partners += [half_group(1), half_group(-1), half_group(2), half_group(-2)]
    barrier = pltpu.get_barrier_semaphore()
    for device in partners:
        pl.semaphore_signal(barrier, inc=1, device_id=device, device_id_type=MESH)
    pl.semaphore_wait(barrier, len(partners))

    mine = px.at[lo, hi, xx, core, par]
    remote(mine, mine, PZ, pair).start()

    def ring_send(d, h, p):
        block = xall.at[origin(d, h - 1), rows_of(p)]
        remote(block, block, ring_id(RING, d, h, p), ahead[d]).start()

    def ring_wait(d, h, p):
        arrived(xall.at[origin(d, h), rows_of(p)], ring_id(RING, d, h, p))

    for p in range(2):
        for d in range(2):
            ring_send(d, 1, p)

    def wq_half(which):
        return wq.at[which, pl.ds(pl.multiple_of(core * (D // 2), D // 2), D // 2)]

    def wkv_half(which):
        return wkv.at[which, pl.ds(pl.multiple_of(core * (D // 2), D // 2), D // 2)]

    def wo_half(which):
        return wo.at[which, pl.ds(pl.multiple_of(core * 128, 128), 128)]

    def sib_rows(ref, size):
        return ref.at[1 - lo, pl.ds(pl.multiple_of((1 - core) * size, size), size)]

    local_wq.wait()
    local_wkv.wait()
    remote(wq_half(lo), wq_half(lo), WY, weight_peer).start()
    remote(wkv_half(lo), wkv_half(lo), WY + 1, weight_peer).start()

    arrived(px.at[lo, hi, xx, core, 1 - par], PZ)
    both = px.at[lo, hi, xx, core]
    remote(both, both, PY, (g, other_t)).start()
    remote(both, both, PY + 1, (other_g, other_t)).start()
    remote(both, both, PY + 2, (other_g, t)).start()

    def ring_step(h):
        for p in range(2):
            for d in range(2):
                if h < 3 or p == d:
                    ring_wait(d, h, p)
                    ring_send(d, h + 1, p)
        if h == 3:
            for d in range(2):
                ring_wait(d, h, 1 - d)

    lane = lax.broadcasted_iota(jnp.int32, (CH, HD), 1)
    low = lane < HD // 2

    def project(c):
        rows = xall[c]
        cosine = cos_ref[c]
        sine = sin_ref[c]
        for y in range(2):
            q_part = jnp.dot(rows, wq[y], preferred_element_type=F32)
            for head in range(2):
                v = q_part[:, head * HD : (head + 1) * HD]
                turned = v * cosine + pltpu.roll(v, HD // 2, 1) * sine
                swapped = pltpu.roll(turned, HD // 2, 1)
                first = jnp.where(low, turned, 0.0)
                second = jnp.where(low, swapped, 0.0)
                qpad[y, c, pl.ds(head * CH, CH), :] = jnp.concatenate([first, second], axis=1).astype(BF)
            kv_part = jnp.dot(rows, wkv[y], preferred_element_type=F32)
            kvs[2, y, par, pl.ds(pl.multiple_of(c * CH, CH), CH)] = kv_part.astype(BF)
        block = kv_rows(par, c)
        remote(block, block, KVZ + c, pair).start()

    def kv_rows(which, c):
        return kvs.at[2, :, which, pl.ds(pl.multiple_of(c * CH, CH), CH)]

    def project_range(first, last):
        def body(k, carry):
            project((z + ((k + 1) // 2) * (2 * (k % 2) - 1) + NZ) % NZ)
            return carry

        lax.fori_loop(first, last, body, 0)

    ring_step(1)
    arrived(px.at[1 - lo, hi, xx, core], PY)
    arrived(px.at[1 - lo, 1 - hi, xx, core], PY + 1)
    arrived(px.at[lo, 1 - hi, xx, core], PY + 2)
    here = px.at[:, :, xx, core]
    for k in range(1, 4):
        remote(here, here, PX + k - 1, along_x(k)).start()
    arrived(wq_half(1 - lo), WY)
    remote(wq_half(1 - lo), wq_half(1 - lo), WSIB, sibling).start()
    arrived(wkv_half(1 - lo), WY + 1)
    remote(wkv_half(1 - lo), wkv_half(1 - lo), WSIB + 1, sibling).start()
    local_wo.wait()
    remote(wo_half(lo), wo_half(lo), WY + 2, weight_peer).start()
    ring_step(2)
    arrived(sib_rows(wq, D // 2), WSIB)
    arrived(sib_rows(wkv, D // 2), WSIB + 1)
    project_range(0, 3)
    ring_step(3)
    for k in range(1, 4):
        arrived(px.at[:, :, (xx + 4 - k) % 4, core], PX + k - 1)
    column = px.at[:, :, :, core]
    remote(column, column, PSIB, sibling).start()
    arrived(wo_half(1 - lo), WY + 2)
    remote(wo_half(1 - lo), wo_half(1 - lo), WSIB + 2, sibling).start()
    project_range(3, 7)
    ring_wait(0, 4, 0)
    ring_wait(1, 4, 1)
    project_range(7, 8)

    def kv_settle(c, carry):
        arrived(kv_rows(1 - par, c), KVZ + c)
        left(kv_rows(par, c), KVZ + c)
        rows = pl.ds(pl.multiple_of(c * CH, CH), CH)
        cosine = jnp.where(low, cos_ref[c], 1.0)
        sine = jnp.where(low, -sin_ref[c], 0.0)
        for y in range(2):
            first = kvs[2, y, 0, rows].astype(F32)
            second = kvs[2, y, 1, rows].astype(F32)
            kvs[2, y, 0, rows] = (first * cosine - second * sine).astype(BF)
            kvs[2, y, 1, rows] = (second * cosine + first * sine).astype(BF)
        return carry

    lax.fori_loop(0, NZ, kv_settle, 0)
    for k in (1, 2):
        remote(kvs.at[2], kvs.at[2 - k], KVH + k - 1, half_group(k)).start()

    def scores_of(queries, keys):
        return lax.dot_general(queries, keys, (((1,), (1,)), ((), ())), preferred_element_type=F32)

    def fold(state, queries, keys, visible):
        scores = jnp.where(visible, scores_of(queries, keys), NEG)
        highest = jnp.max(scores, axis=-1, keepdims=True)
        if state is None:
            top = highest
        else:
            top = jnp.maximum(state[0], highest)
        weights = jnp.exp2((scores - top) * SCALE)
        total = jnp.sum(weights, axis=-1, keepdims=True)
        acc = jnp.dot(weights.astype(BF), keys, preferred_element_type=F32)
        if state is None:
            return (top, total, acc)
        factor = jnp.exp2((state[0] - top) * SCALE)
        return (top, state[1] * factor + total, state[2] * factor + acc)

    def offsets(c):
        one = off_ref[c]
        return jnp.concatenate([one, one], axis=0)

    def prefix_part(c):
        offset = offsets(c)
        for y in range(2):
            queries = qpad[y, c]
            state = None
            for b in range(4):
                parts = []
                for k in range(4):
                    at = (y, b // 2, (b % 2) * 2 + k // 2, k % 2)
                    parts.append(jnp.concatenate([px[at + (0,)], px[at + (1,)]], axis=1))
                keys = jnp.concatenate(parts, axis=0)
                state = fold(state, queries, keys, kpe_ref[b] > offset)
            st_m[c, y] = state[0]
            st_l[c, y] = state[1]
            st_acc[c, y] = state[2]

    def suffix_part(c):
        offset = offsets(c)
        row = lax.broadcasted_iota(jnp.int32, (2 * CH, 1), 0) % CH + c * CH
        row = row.astype(F32)
        column_index = lax.broadcasted_iota(jnp.int32, (1, HALF), 1).astype(F32)
        for y in range(2):
            queries = qpad[y, c]
            state = (st_m[c, y], st_l[c, y], st_acc[c, y])
            for slot in range(3):
                keys = jnp.concatenate([kvs[slot, y, 0], kvs[slot, y, 1]], axis=1)
                index = column_index + (slot - 2) * HALF
                visible = (index >= row - offset) & (index <= row)
                state = fold(state, queries, keys, visible)
            result = state[2] / state[1]
            first = pltpu.roll(result[:, :HD], HD // 2, 1)
            lane2 = lax.broadcasted_iota(jnp.int32, (2 * CH, HD), 1)
            merged = jnp.where(lane2 < HD // 2, first, result[:, HD:]).astype(BF)
            attn[:, pl.ds(y * 256, HD)] = merged[:CH]
            attn[:, pl.ds(y * 256 + HD, HD)] = merged[CH:]

    tile = 1024

    def out_tile(n):
        cols = pl.ds(pl.multiple_of(n * tile, tile), tile)
        rows = attn[...]
        term = jnp.dot(rows[:, :256], wo[0, :, cols], preferred_element_type=F32)
        return cols, term + jnp.dot(rows[:, 256:], wo[1, :, cols], preferred_element_type=F32)

    def chunk_of(i):
        h = (8 - i) // 2
        return (z + h * (2 * (i % 2) - 1) + NZ) % NZ

    arrived(px.at[:, :, :, 1 - core], PSIB)

    def early(i, carry):
        prefix_part(chunk_of(i))
        return carry

    lax.fori_loop(0, 3, early, 0)
    for k in (1, 2):
        arrived(kvs.at[2 - k], KVH + k - 1)
    arrived(sib_rows(wo, 128), WSIB + 2)

    def rs_send(d, h, p):
        to = (g, lo * NZ + (z + 1 - 2 * d + NZ) % NZ)
        src = sbuf.at[d, h - 1, rows_of(p)]
        dst = rbuf.at[d, h - 1, rows_of(p)]
        remote(src, dst, ring_id(RS, d, h, p), to).start()

    def rs_wait(d, h, p):
        arrived(rbuf.at[d, h - 1, rows_of(p)], ring_id(RS, d, h, p))

    def reduce_step(i, carry):
        h = (8 - i) // 2
        d = (i + 1) % 2
        c = chunk_of(i)

        @pl.when(i >= 3)
        def _():
            prefix_part(c)

        suffix_part(c)

        @pl.when(i == 0)
        def _():
            @pl.loop(0, D // tile)
            def _(n):
                cols, term = out_tile(n)
                sbuf[0, 3, rows_of(0), cols] = term[:32].astype(BF)
                sbuf[1, 3, rows_of(1), cols] = term[32:].astype(BF)

            rs_send(0, 4, 0)
            rs_send(1, 4, 1)

        @pl.when((i > 0) & (i < 3))
        def _():
            rs_wait(d, 4, d)

        @pl.when(i >= 3)
        def _():
            @pl.when(i < 7)
            def _():
                for p in range(2):
                    rs_wait(d, h + 1, p)

        @pl.when((i > 0) & (i < 7))
        def _():
            @pl.loop(0, D // tile)
            def _(n):
                cols, term = out_tile(n)
                sbuf[d, h - 1, :, cols] = (term + rbuf[d, h, :, cols].astype(F32)).astype(BF)

            for p in range(2):
                rs_send(d, h, p)

        @pl.when(i == 7)
        def _():
            for dd in range(2):
                for p in range(2):
                    rs_wait(dd, 1, p)

            @pl.loop(0, D // tile)
            def _(n):
                cols, term = out_tile(n)
                term = term + rbuf[0, 0, :, cols].astype(F32) + rbuf[1, 0, :, cols].astype(F32)
                out_ref[:, cols] = term.astype(BF)

        return carry

    lax.fori_loop(0, 8, reduce_step, 0)

    left(mine, PZ)
    for k in range(3):
        left(both, PY + k)
        left(here, PX + k)
    left(column, PSIB)
    for k, half in enumerate((wq_half, wkv_half, wo_half)):
        left(half(lo), WY + k)
        left(half(1 - lo), WSIB + k)
    for k in range(2):
        left(kvs.at[2], KVH + k)
    for d in range(2):
        for h in range(1, 5):
            for p in range(2):
                if h < 4 or p == d:
                    left(xall.at[0, rows_of(p)], ring_id(RING, d, h, p))
                    left(sbuf.at[d, h - 1, rows_of(p)], ring_id(RS, d, h, p))


def local(x_rows, norm_gain, w_query, w_keyval, w_out, prefix_cache, page_table, request_ids):
    half_start = lax.axis_index("grp") * (2 * HALF) + (lax.axis_index("tp") // NZ) * HALF
    padded = jnp.concatenate([jnp.full((2 * HALF,), -1, jnp.int32), request_ids])
    window = lax.dynamic_slice_in_dim(padded, half_start, 3 * HALF, 0)
    own = lax.dynamic_slice_in_dim(request_ids, half_start, HALF, 0)
    earlier = jnp.arange(3 * HALF)[None, :] < jnp.arange(HALF)[:, None] + 2 * HALF
    offset = jnp.sum(((window[None, :] == own[:, None]) & earlier).astype(jnp.int32), axis=1)
    freqs = 500000.0 ** (-jnp.arange(HD // 2, dtype=F32) * 2.0 / HD)
    angles = (PREFIX + offset).astype(F32)[:, None] * freqs[None, :]
    cosine = jnp.cos(angles)
    sine = jnp.sin(angles)
    cos2 = jnp.concatenate([cosine, cosine], axis=1).reshape(NZ, CH, HD)
    sin2 = jnp.concatenate([-sine, sine], axis=1).reshape(NZ, CH, HD)
    pages = page_table.shape[0]
    labels = jnp.arange(pages, dtype=jnp.int32)
    logical = jnp.sum(jnp.where(page_table[None, :] == labels[:, None], labels[None, :], 0), axis=1)
    key_pos = logical[:, None] * HD + jnp.arange(HD, dtype=jnp.int32)[None, :]
    key_pos = jnp.where(key_pos < SINKS, 1 << 20, key_pos).astype(F32).reshape(4, 1, 1024)

    vmem = pl.BlockSpec(memory_space=pltpu.VMEM)
    hbm = pl.BlockSpec(memory_space=pl.ANY)
    return pl.pallas_call(
        kernel,
        out_shape=jax.ShapeDtypeStruct((CH, D), BF),
        in_specs=[vmem] * 7 + [hbm] * 3,
        out_specs=vmem,
        scratch_shapes=[
            pltpu.VMEM((NZ, CH, D), BF),
            pltpu.VMEM((2, D, 256), BF),
            pltpu.VMEM((2, D, 128), BF),
            pltpu.VMEM((2, 256, D), BF),
            pltpu.VMEM((2, 2, 4, 2, 2, 256, 128), BF),
            pltpu.VMEM((3, 2, 2, HALF, 128), BF),
            pltpu.VMEM((2, NZ, 2 * CH, 256), BF),
            pltpu.VMEM((NZ, 2, 2 * CH, 1), F32),
            pltpu.VMEM((NZ, 2, 2 * CH, 1), F32),
            pltpu.VMEM((NZ, 2, 2 * CH, 256), F32),
            pltpu.VMEM((CH, 512), BF),
            pltpu.VMEM((2, 4, CH, D), BF),
            pltpu.VMEM((2, 4, CH, D), BF),
            pltpu.SemaphoreType.DMA((MESSAGES,)),
            pltpu.SemaphoreType.DMA((MESSAGES,)),
            pltpu.SemaphoreType.DMA((3,)),
        ],
        compiler_params=pltpu.CompilerParams(
            collective_id=0, has_side_effects=True, vmem_limit_bytes=60 << 20
        ),
    )(
        x_rows,
        norm_gain.reshape(1, D),
        prefix_cache.reshape(256, 128),
        key_pos,
        offset.astype(F32).reshape(NZ, CH, 1),
        cos2,
        sin2,
        w_query,
        w_keyval.reshape(D, 128),
        w_out,
    )


def solution(mesh):
    placed = (
        P(("grp", "tp"), None),
        P(),
        P(None, "tp"),
        P(None, None, "tp"),
        P("tp", None),
        P("grp", None, None, "tp"),
        P(),
        P(),
    )
    return jax.shard_map(
        local, mesh=mesh, in_specs=placed, out_specs=P(("grp", "tp"), None), check_vma=False
    )
```

time: 374 us -> 158 us (0.42)
  the two profiles are of different devices: /device:TPU:1 before, /device:TPU:16 now
where the time goes in v1:
time: 158 us
  Pallas kernels  146 us (92%)
  local copies, waits for them, and re-layouts  7.57 us (5%)
  other arithmetic  4.35 us (3%)
    pallas_call x1, Pallas kernels, local(): pl.pallas_call(kernel, out_shape=jax.ShapeDtypeStruct((CH, D), BF), in_sp...  146 us

profile of v1, /device:TPU:16, one launch (start us, length us, event | category | flops | bytes accessed | tf_op | source)
XLA Modules:
  0.0 157.6 jit_solution(11980666922837861880)
XLA Ops:
  0.0 0.0 copy-start
  0.0 0.9 select_reduce_fusion
  0.9 0.1 mul.42
  1.0 0.8 dynamic_slice.7
  1.7 0.8 pad_dynamic-slice_fusion
  2.5 0.8 convert_reduce_fusion
  3.4 0.1 convert_element_type.41
  3.4 0.1 add.60
  3.5 0.6 fusion.2.kpe_ref
  4.1 1.0 copy.19
  5.1 0.7 reshape.148.pre_ref
  5.8 0.9 convert_element_type.42.off_ref
  6.7 1.0 fusion.1
  7.7 1.0 pad_maximum_fusion
  8.8 0.0 copy-done
  8.8 1.3 copy.18.wkv_ref
  10.1 145.7 %shard_map.82 = bf16[64,4096]{1,0:T(8,128)(2,1)} custom-call(bf16[64,4096]{1,0:T(8,128)(2,1)} %x_ref.1, f32[1,4096]{1,0:T(1,128)} %bitcast.7, bf16[256,128]{1,0:T(8,128)(2,1)} %reshape.148.pre_ref, f32[4,1,1024]{2,1,0:T(1,128)} %fusion.2.kpe_ref, f32[8,64,1]{2,1,0:T(8,128)} %convert_element_type.42.off_ref, f32[8,64,128]{2,1,0:T(8,128)} %get-tuple-element.10.cos_ref, ...), custom_call_target="tpu_custom_call" | custom-call | tf_op jit(solution)/shard_map/pallas_call | solution.py:441
  155.8 1.9 %copy.22 = bf16[64,4096]{1,0:T(8,128)(2,1)} copy(bf16[64,4096]{1,0:T(8,128)(2,1)} %shard_map.82) | data formatting | bytes 1048576
  (5 shorter events, 0.0 us)
Async XLA Ops:
  0.0 8.8 %copy-start = (bf16[4096,2,64]{0,2,1:T(8,128)(2,1)S(1)}, bf16[4096,2,64]{0,2,1:T(8,128)(2,1)}, u32[]{:S(2)}) copy-start(bf16[4096,2,64]{0,2,1:T(8,128)(2,1)} %param.11) | copy-start | bytes 3145732

commit v2 on v1

v2 whole, which is shorter than its diff:
```python
import math

import jax
import jax.numpy as jnp
import numpy as np
from jax import lax
from jax.experimental import pallas as pl
from jax.experimental.pallas import tpu as pltpu
from jax.sharding import PartitionSpec as P

MESH = pl.DeviceIdType.MESH
HD = 128
SINKS = 4
D = 4096
CH = 64
NZ = 8
HALF = CH * NZ
PREFIX = 4096
SCALE = HD**-0.5 * math.log2(math.e)
NEG = -1e30
BF = jnp.bfloat16
F32 = jnp.float32

RING, PZ, PY, PX, PSIB, WY, WSIB, KVZ, KVH, RS = 0, 16, 17, 20, 23, 24, 27, 30, 38, 54
MESSAGES = 70


def ring_id(base, d, h, p):
    return base + (d * 4 + (h - 1)) * 2 + p


def kernel(
    x_ref,
    gain_ref,
    pre_ref,
    ids_ref,
    freq_ref,
    pages_ref,
    wq_ref,
    wkv_ref,
    wo_ref,
    out_ref,
    xall,
    wq,
    wkv,
    wo,
    px,
    kvs,
    qpad,
    st_m,
    st_l,
    st_acc,
    attn,
    kpe,
    off,
    cosines,
    sines,
    tbuf,
    sbuf,
    rbuf,
    ssem,
    rsem,
    lsem,
):
    g = lax.axis_index("grp")
    t = lax.axis_index("tp")
    core = g % 2
    xx = (g // 2) % 4
    hi = g // 8
    z = t % NZ
    lo = t // NZ
    par = z % 2
    up = (g, lo * NZ + (z + 1) % NZ)
    down = (g, lo * NZ + (z + NZ - 1) % NZ)
    pair = (g, t + 1 - 2 * par)
    other_t = (1 - lo) * NZ + z
    other_g = (1 - hi) * 8 + xx * 2 + core
    sibling = (g + 1 - 2 * core, t)
    weight_peer = (core * other_g + (1 - core) * g, other_t)

    def along_x(k):
        return (hi * 8 + ((xx + k) % 4) * 2 + core, t)

    def half_group(k):
        index = (2 * g + lo + k + 32) % 32
        return (index // 2, (index % 2) * NZ + z)

    def remote(src, dst, number, device):
        return pltpu.make_async_remote_copy(
            src_ref=src,
            dst_ref=dst,
            send_sem=ssem.at[number],
            recv_sem=rsem.at[number],
            device_id=device,
            device_id_type=MESH,
        )

    def arrived(ref, number):
        remote(ref, ref, number, sibling).wait_recv()

    def left(ref, number):
        remote(ref, ref, number, sibling).wait_send()

    ahead = (up, down)
    sign = (1, -1)

    def rows_of(p):
        return pl.ds(p * 32, 32)

    def origin(d, h):
        return (z - sign[d] * h + NZ) % NZ

    local_wq = pltpu.make_async_copy(wq_ref, wq.at[lo], lsem.at[0])
    local_wkv = pltpu.make_async_copy(wkv_ref, wkv.at[lo], lsem.at[1])
    local_wo = pltpu.make_async_copy(wo_ref, wo.at[lo], lsem.at[2])
    local_wq.start()
    local_wkv.start()
    local_wo.start()
    wide = x_ref[...].astype(F32)
    variance = jnp.mean(wide * wide, axis=-1, keepdims=True) + 1e-05
    xall[z] = (wide * lax.rsqrt(variance) * gain_ref[...]).astype(BF)
    for page in range(2):
        rows = pl.ds(page * 128, 128)
        px[lo, hi, xx, core, par, rows, :] = pre_ref[rows, :].astype(F32).T.astype(BF)
    for d in range(2):
        rbuf[d, 3, rows_of(1 - d)] = jnp.zeros((32, D), BF)

    partners = [up, down, (g, other_t), (other_g, other_t), (other_g, t)]
    partners += [along_x(1), along_x(2), along_x(3), sibling]
    partners += [half_group(1), half_group(-1), half_group(2), half_group(-2)]
    barrier = pltpu.get_barrier_semaphore()
    for device in partners:
        pl.semaphore_signal(barrier, inc=1, device_id=device, device_id_type=MESH)
    pl.semaphore_wait(barrier, len(partners))

    mine = px.at[lo, hi, xx, core, par]
    remote(mine, mine, PZ, pair).start()

    def ring_send(d, h, p):
        block = xall.at[origin(d, h - 1), rows_of(p)]
        remote(block, block, ring_id(RING, d, h, p), ahead[d]).start()

    def ring_wait(d, h, p):
        arrived(xall.at[origin(d, h), rows_of(p)], ring_id(RING, d, h, p))

    for p in range(2):
        for d in range(2):
            ring_send(d, 1, p)

    def wq_half(which):
        return wq.at[which, pl.ds(pl.multiple_of(core * (D // 2), D // 2), D // 2)]

    def wkv_half(which):
        return wkv.at[which, pl.ds(pl.multiple_of(core * 64, 64), 64)]

    def wo_half(which):
        return wo.at[which, pl.ds(pl.multiple_of(core * 128, 128), 128)]

    def sib_rows(ref, size):
        return ref.at[1 - lo, pl.ds(pl.multiple_of((1 - core) * size, size), size)]

    local_wq.wait()
    local_wkv.wait()
    remote(wq_half(lo), wq_half(lo), WY, weight_peer).start()
    remote(wkv_half(lo), wkv_half(lo), WY + 1, weight_peer).start()

    arrived(px.at[lo, hi, xx, core, 1 - par], PZ)
    both = px.at[lo, hi, xx, core]
    remote(both, both, PY, (g, other_t)).start()
    remote(both, both, PY + 1, (other_g, other_t)).start()
    remote(both, both, PY + 2, (other_g, t)).start()

    def ring_step(h):
        for p in range(2):
            for d in range(2):
                if h < 3 or p == d:
                    ring_wait(d, h, p)
                    ring_send(d, h + 1, p)
        if h == 3:
            for d in range(2):
                ring_wait(d, h, 1 - d)

    lane = lax.broadcasted_iota(jnp.int32, (CH, HD), 1)
    low = lane < HD // 2

    def project(c, y):
        rows = xall[c]
        cosine = cosines[c]
        sine = sines[c]
        q_part = jnp.dot(rows, wq[y], preferred_element_type=F32)
        for head in range(2):
            v = q_part[:, head * HD : (head + 1) * HD]
            turned = v * cosine + pltpu.roll(v, HD // 2, 1) * sine
            swapped = pltpu.roll(turned, HD // 2, 1)
            first = jnp.where(low, turned, 0.0)
            second = jnp.where(low, swapped, 0.0)
            qpad[y, c, pl.ds(head * CH, CH), :] = jnp.concatenate([first, second], axis=1).astype(BF)
        kv_part = scores_of(rows, wkv[y])
        kvs[2, y, par, pl.ds(pl.multiple_of(c * CH, CH), CH)] = kv_part.astype(BF)

    def scores_of(queries, keys):
        return lax.dot_general(queries, keys, (((1,), (1,)), ((), ())), preferred_element_type=F32)

    def kv_rows(which, c):
        return kvs.at[2, :, which, pl.ds(pl.multiple_of(c * CH, CH), CH)]

    def in_order(k):
        return (z + ((k + 1) // 2) * (2 * (k % 2) - 1) + NZ) % NZ

    def project_own(first, last):
        def body(k, carry):
            project(in_order(k), lo)
            return carry

        lax.fori_loop(first, last, body, 0)

    def project_other(first, last):
        def body(k, carry):
            c = in_order(k)
            project(c, 1 - lo)
            block = kv_rows(par, c)
            remote(block, block, KVZ + c, pair).start()
            return carry

        lax.fori_loop(first, last, body, 0)

    pieces = []
    for k in range(3):
        block = 2 * g + lo - 2 + k
        for r in range(4):
            ids = ids_ref[pl.ds(jnp.maximum(block, 0) * 4 + r, 1), :].astype(F32)
            pieces.append(jnp.where(block >= 0, ids, -1.0))
    window = jnp.concatenate(pieces, axis=1)

    def tables(c, carry):
        row = lax.broadcasted_iota(jnp.int32, (CH, 3 * HALF), 0) + c * CH + 2 * HALF
        col = lax.broadcasted_iota(jnp.int32, (CH, 3 * HALF), 1)
        own = jnp.sum(jnp.where(col == row, window, 0.0), axis=1, keepdims=True)
        earlier = (window == own) & (col < row)
        offset = jnp.sum(jnp.where(earlier, 1.0, 0.0), axis=1, keepdims=True)
        off[c] = offset
        angles = (PREFIX + offset) * freq_ref[...]
        sine = jnp.sin(angles)
        cosines[c] = jnp.cos(angles)
        sines[c] = jnp.where(low, -sine, sine)
        return carry

    lax.fori_loop(0, NZ, tables, 0)
    page_row = lax.broadcasted_iota(jnp.int32, (32, 128), 0)
    logical = jnp.zeros((32, 128), F32)
    for page in range(32):
        logical = logical + jnp.where(page_row == pages_ref[page], float(page), 0.0)
    key_pos = logical * 128.0 + lax.broadcasted_iota(jnp.int32, (32, 128), 1).astype(F32)
    kpe[...] = jnp.where(key_pos < SINKS, 1e6, key_pos)
    project_own(0, 1)

    def kv_settle(c):
        arrived(kv_rows(1 - par, c), KVZ + c)
        left(kv_rows(par, c), KVZ + c)
        rows = pl.ds(pl.multiple_of(c * CH, CH), CH)
        cosine = jnp.where(low, cosines[c], 1.0)
        sine = jnp.where(low, -sines[c], 0.0)
        for y in range(2):
            first = kvs[2, y, 0, rows].astype(F32)
            second = kvs[2, y, 1, rows].astype(F32)
            kvs[2, y, 0, rows] = (first * cosine - second * sine).astype(BF)
            kvs[2, y, 1, rows] = (second * cosine + first * sine).astype(BF)
        for k in (1, 2):
            remote(kv_chunk(2, c), kv_chunk(2 - k, c), KVH + 2 * c + k - 1, half_group(k)).start()

    def kv_chunk(slot, c):
        return kvs.at[slot, :, :, pl.ds(pl.multiple_of(c * CH, CH), CH)]

    def settle(first, last):
        def body(k, carry):
            kv_settle(in_order(k))
            return carry

        lax.fori_loop(first, last, body, 0)

    def fold(state, queries, keys, visible):
        scores = jnp.where(visible, scores_of(queries, keys), NEG)
        highest = jnp.max(scores, axis=-1, keepdims=True)
        if state is None:
            top = highest
        else:
            top = jnp.maximum(state[0], highest)
        weights = jnp.exp2((scores - top) * SCALE)
        total = jnp.sum(weights, axis=-1, keepdims=True)
        acc = jnp.dot(weights.astype(BF), keys, preferred_element_type=F32)
        if state is None:
            return (top, total, acc)
        factor = jnp.exp2((state[0] - top) * SCALE)
        return (top, state[1] * factor + total, state[2] * factor + acc)

    def offsets(c):
        one = off[c]
        return jnp.concatenate([one, one], axis=0)

    def prefix_part(c):
        offset = offsets(c)
        for y in range(2):
            queries = qpad[y, c]
            state = None
            for b in range(4):
                parts = []
                for k in range(4):
                    at = (y, b // 2, (b % 2) * 2 + k // 2, k % 2)
                    parts.append(jnp.concatenate([px[at + (0,)], px[at + (1,)]], axis=1))
                keys = jnp.concatenate(parts, axis=0)
                positions = jnp.concatenate([kpe[pl.ds(8 * b + r, 1), :] for r in range(8)], axis=1)
                state = fold(state, queries, keys, positions > offset)
            st_m[c, y] = state[0]
            st_l[c, y] = state[1]
            st_acc[c, y] = state[2]

    def suffix_part(c, slot_out):
        offset = offsets(c)
        row = lax.broadcasted_iota(jnp.int32, (2 * CH, 1), 0) % CH + c * CH
        row = row.astype(F32)
        column_index = lax.broadcasted_iota(jnp.int32, (1, HALF), 1).astype(F32)
        for y in range(2):
            queries = qpad[y, c]
            state = (st_m[c, y], st_l[c, y], st_acc[c, y])
            for slot in range(3):
                keys = jnp.concatenate([kvs[slot, y, 0], kvs[slot, y, 1]], axis=1)
                index = column_index + (slot - 2) * HALF
                visible = (index >= row - offset) & (index <= row)
                state = fold(state, queries, keys, visible)
            result = state[2] / state[1]
            first = pltpu.roll(result[:, :HD], HD // 2, 1)
            lane2 = lax.broadcasted_iota(jnp.int32, (2 * CH, HD), 1)
            merged = jnp.where(lane2 < HD // 2, first, result[:, HD:]).astype(BF)
            attn[slot_out, :, pl.ds(y * 256, HD)] = merged[:CH]
            attn[slot_out, :, pl.ds(y * 256 + HD, HD)] = merged[CH:]

    tile = 1024

    def out_terms(slot):
        @pl.loop(0, D // tile)
        def _(n):
            cols = pl.ds(pl.multiple_of(n * tile, tile), tile)
            rows = attn[slot]
            term = jnp.dot(rows[:, :256], wo[0, :, cols], preferred_element_type=F32)
            tbuf[slot, :, cols] = term + jnp.dot(rows[:, 256:], wo[1, :, cols], preferred_element_type=F32)

    def rs_send(d, h, p):
        src = sbuf.at[d, h - 1, rows_of(p)]
        dst = rbuf.at[d, h - 1, rows_of(p)]
        remote(src, dst, ring_id(RS, d, h, p), ahead[d]).start()

    def rs_wait(d, h, p):
        arrived(rbuf.at[d, h - 1, rows_of(p)], ring_id(RS, d, h, p))

    ring_step(1)
    arrived(px.at[1 - lo, hi, xx, core], PY)
    arrived(px.at[1 - lo, 1 - hi, xx, core], PY + 1)
    arrived(px.at[lo, 1 - hi, xx, core], PY + 2)
    here = px.at[:, :, xx, core]
    for k in range(1, 4):
        remote(here, here, PX + k - 1, along_x(k)).start()
    project_own(1, 3)
    ring_step(2)
    arrived(wq_half(1 - lo), WY)
    remote(wq_half(1 - lo), wq_half(1 - lo), WSIB, sibling).start()
    arrived(wkv_half(1 - lo), WY + 1)
    remote(wkv_half(1 - lo), wkv_half(1 - lo), WSIB + 1, sibling).start()
    local_wo.wait()
    remote(wo_half(lo), wo_half(lo), WY + 2, weight_peer).start()
    project_own(3, 5)
    arrived(sib_rows(wq, D // 2), WSIB)
    arrived(sib_rows(wkv, 64), WSIB + 1)
    project_other(0, 5)
    ring_step(3)
    for k in range(1, 4):
        arrived(px.at[:, :, (xx + 4 - k) % 4, core], PX + k - 1)
    column = px.at[:, :, :, core]
    remote(column, column, PSIB, sibling).start()
    project_own(5, 7)
    project_other(5, 7)
    settle(0, 5)
    ring_wait(0, 4, 0)
    ring_wait(1, 4, 1)
    project_own(7, 8)
    project_other(7, 8)
    arrived(wo_half(1 - lo), WY + 2)
    remote(wo_half(1 - lo), wo_half(1 - lo), WSIB + 2, sibling).start()
    arrived(px.at[:, :, :, 1 - core], PSIB)

    def early(k, carry):
        prefix_part(in_order(k))
        return carry

    lax.fori_loop(7, 8, early, 0)
    settle(5, 8)
    lax.fori_loop(5, 7, early, 0)

    def kv_arrive(c, carry):
        for k in (1, 2):
            arrived(kv_chunk(2 - k, c), KVH + 2 * c + k - 1)
        return carry

    lax.fori_loop(0, NZ, kv_arrive, 0)
    arrived(sib_rows(wo, 128), WSIB + 2)

    col_tiles = [pl.ds(n * tile, tile) for n in range(D // tile)]
    suffix_part((z + 4) % NZ, 0)
    out_terms(0)
    for d in range(2):
        for cols in col_tiles:
            sbuf[d, 3, rows_of(d), cols] = tbuf[0, rows_of(d), cols].astype(BF)
        rs_send(d, 4, d)

    def reduce_step(i, carry):
        h = 3 - i

        def terms(d, carry):
            c = (z + (1 - 2 * d) * h + NZ) % NZ

            @pl.when(i > 0)
            def _():
                prefix_part(c)

            suffix_part(c, d)
            out_terms(d)
            return carry

        lax.fori_loop(0, 2, terms, 0)
        for fresh in (True, False):
            for d in range(2):
                p = 1 - d if fresh else d
                if fresh:

                    @pl.when(i > 0)
                    def _():
                        rs_wait(d, h + 1, p)

                else:
                    rs_wait(d, h + 1, p)
                for cols in col_tiles:
                    total = tbuf[d, rows_of(p), cols] + rbuf[d, h, rows_of(p), cols].astype(F32)
                    sbuf[d, h - 1, rows_of(p), cols] = total.astype(BF)
                rs_send(d, h, p)
        return carry

    lax.fori_loop(0, 3, reduce_step, 0)
    prefix_part(z)
    suffix_part(z, 0)
    out_terms(0)
    for p in range(2):
        for d in range(2):
            rs_wait(d, 1, p)
        for cols in col_tiles:
            total = tbuf[0, rows_of(p), cols] + rbuf[0, 0, rows_of(p), cols].astype(F32)
            out_ref[rows_of(p), cols] = (total + rbuf[1, 0, rows_of(p), cols].astype(F32)).astype(BF)

    left(mine, PZ)
    for k in range(3):
        left(both, PY + k)
        left(here, PX + k)
    left(column, PSIB)
    for k, half in enumerate((wq_half, wkv_half, wo_half)):
        left(half(lo), WY + k)
        left(half(1 - lo), WSIB + k)

    def kv_left(c, carry):
        for k in (1, 2):
            left(kv_chunk(2, c), KVH + 2 * c + k - 1)
        return carry

    lax.fori_loop(0, NZ, kv_left, 0)
    for d in range(2):
        for h in range(1, 5):
            for p in range(2):
                if h < 4 or p == d:
                    left(xall.at[0, rows_of(p)], ring_id(RING, d, h, p))
                    left(sbuf.at[d, h - 1, rows_of(p)], ring_id(RS, d, h, p))


def local(x_rows, norm_gain, w_query, w_keyval, w_out, prefix_cache, page_table, request_ids):
    exponents = -(np.arange(HD) % (HD // 2)) * 2.0 / HD
    freqs = jnp.asarray((500000.0**exponents).astype(np.float32)).reshape(1, HD)
    vmem = pl.BlockSpec(memory_space=pltpu.VMEM)
    hbm = pl.BlockSpec(memory_space=pl.ANY)
    return pl.pallas_call(
        kernel,
        out_shape=jax.ShapeDtypeStruct((CH, D), BF),
        in_specs=[vmem] * 5 + [pl.BlockSpec(memory_space=pltpu.SMEM)] + [hbm] * 3,
        out_specs=vmem,
        scratch_shapes=[
            pltpu.VMEM((NZ, CH, D), BF),
            pltpu.VMEM((2, D, 256), BF),
            pltpu.VMEM((2, 128, D), BF),
            pltpu.VMEM((2, 256, D), BF),
            pltpu.VMEM((2, 2, 4, 2, 2, 256, 128), BF),
            pltpu.VMEM((3, 2, 2, HALF, 128), BF),
            pltpu.VMEM((2, NZ, 2 * CH, 256), BF),
            pltpu.VMEM((NZ, 2, 2 * CH, 1), F32),
            pltpu.VMEM((NZ, 2, 2 * CH, 1), F32),
            pltpu.VMEM((NZ, 2, 2 * CH, 256), F32),
            pltpu.VMEM((2, CH, 512), BF),
            pltpu.VMEM((32, 128), F32),
            pltpu.VMEM((NZ, CH, 1), F32),
            pltpu.VMEM((NZ, CH, HD), F32),
            pltpu.VMEM((NZ, CH, HD), F32),
            pltpu.VMEM((2, CH, D), F32),
            pltpu.VMEM((2, 4, CH, D), BF),
            pltpu.VMEM((2, 4, CH, D), BF),
            pltpu.SemaphoreType.DMA((MESSAGES,)),
            pltpu.SemaphoreType.DMA((MESSAGES,)),
            pltpu.SemaphoreType.DMA((3,)),
        ],
        compiler_params=pltpu.CompilerParams(
            collective_id=0, has_side_effects=True, vmem_limit_bytes=60 << 20
        ),
    )(
        x_rows,
        norm_gain.reshape(1, D),
        prefix_cache.transpose(0, 2, 3, 1).reshape(256, 128),
        request_ids.reshape(128, 128),
        freqs,
        page_table,
        w_query,
        w_keyval.transpose(1, 2, 0).reshape(128, D),
        w_out,
    )


def solution(mesh):
    placed = (
        P(("grp", "tp"), None),
        P(),
        P(None, "tp"),
        P(None, None, "tp"),
        P("tp", None),
        P("grp", None, None, "tp"),
        P(),
        P(),
    )
    return jax.shard_map(
        local, mesh=mesh, in_specs=placed, out_specs=P(("grp", "tp"), None), check_vma=False
    )
```

time: 158 us -> 136 us (0.86)
  the two profiles are of different devices: /device:TPU:16 before, /device:TPU:1 now
where the time goes in v2:
time: 136 us; the launch traced here: 135 us
  Pallas kernels  133 us (98%)
  local copies, waits for them, and re-layouts  1.87 us (1%)
    pallas_call x1, Pallas kernels, local(): pl.pallas_call(kernel, out_shape=jax.ShapeDtypeStruct((CH, D), BF), in_sp...  133 us

profile of v2, /device:TPU:1, one launch (start us, length us, event | category | flops | bytes accessed | tf_op | source)
XLA Modules:
  0.0 135.0 jit_solution(13765189552227390042)
XLA Ops:
  0.0 133.1 %shard_map.91 = bf16[64,4096]{1,0:T(8,128)(2,1)} custom-call(bf16[64,4096]{1,0:T(8,128)(2,1)} %x_ref.1, f32[1,4096]{1,0:T(1,128)} %bitcast.11, bf16[256,128]{1,0:T(8,128)(2,1)} %bitcast.9, s32[128,128]{1,0:T(8,128)} %bitcast.10, f32[1,128]{1,0:T(1,128)} %constant.5.freq_ref, s32[32]{0:T(128)} %pages_ref.1, bf16[4096,256]{1,0:T(8,128)(2,1)} %wq_ref.1, ...), custom_call_target="tpu_custom_call" | custom-call | tf_op jit(solution)/shard_map/pallas_call | solution.py:485
  133.1 1.9 %copy.11 = bf16[64,4096]{1,0:T(8,128)(2,1)} copy(bf16[64,4096]{1,0:T(8,128)(2,1)} %shard_map.91) | data formatting | bytes 1048576

commit v3 on v2

--- a/solution.py
+++ b/solution.py
@@ -21,8 +21,8 @@
 BF = jnp.bfloat16
 F32 = jnp.float32
 
-RING, PZ, PY, PX, PSIB, WY, WSIB, KVZ, KVH, RS = 0, 16, 17, 20, 23, 24, 27, 30, 38, 54
-MESSAGES = 70
+RING, PZ, PY, PX, PSIB, WY, WSIB, KVZ, KVH, RS = 0, 16, 17, 20, 24, 25, 28, 31, 39, 55
+MESSAGES = 71
 
 
 def ring_id(base, d, h, p):
@@ -126,7 +126,7 @@
         rbuf[d, 3, rows_of(1 - d)] = jnp.zeros((32, D), BF)
 
     partners = [up, down, (g, other_t), (other_g, other_t), (other_g, t)]
-    partners += [along_x(1), along_x(2), along_x(3), sibling]
+    partners += [along_x(1), along_x(3), sibling]
     partners += [half_group(1), half_group(-1), half_group(2), half_group(-2)]
     barrier = pltpu.get_barrier_semaphore()
     for device in partners:
@@ -158,11 +158,6 @@
 
     def sib_rows(ref, size):
         return ref.at[1 - lo, pl.ds(pl.multiple_of((1 - core) * size, size), size)]
-
-    local_wq.wait()
-    local_wkv.wait()
-    remote(wq_half(lo), wq_half(lo), WY, weight_peer).start()
-    remote(wkv_half(lo), wkv_half(lo), WY + 1, weight_peer).start()
 
     arrived(px.at[lo, hi, xx, core, 1 - par], PZ)
     both = px.at[lo, hi, xx, core]
@@ -183,20 +178,26 @@
     lane = lax.broadcasted_iota(jnp.int32, (CH, HD), 1)
     low = lane < HD // 2
 
-    def project(c, y):
-        rows = xall[c]
-        cosine = cosines[c]
-        sine = sines[c]
+    def project_kv(chunks, y):
+        rows = jnp.concatenate([xall[c] for c in chunks], axis=0)
+        kv_part = scores_of(rows, wkv[y]).astype(BF)
+        for n, c in enumerate(chunks):
+            kvs[2, y, par, pl.ds(pl.multiple_of(c * CH, CH), CH)] = kv_part[n * CH : (n + 1) * CH]
+
+    def project_q(chunks, y):
+        rows = jnp.concatenate([xall[c] for c in chunks], axis=0)
         q_part = jnp.dot(rows, wq[y], preferred_element_type=F32)
-        for head in range(2):
-            v = q_part[:, head * HD : (head + 1) * HD]
-            turned = v * cosine + pltpu.roll(v, HD // 2, 1) * sine
-            swapped = pltpu.roll(turned, HD // 2, 1)
-            first = jnp.where(low, turned, 0.0)
-            second = jnp.where(low, swapped, 0.0)
-            qpad[y, c, pl.ds(head * CH, CH), :] = jnp.concatenate([first, second], axis=1).astype(BF)
-        kv_part = scores_of(rows, wkv[y])
-        kvs[2, y, par, pl.ds(pl.multiple_of(c * CH, CH), CH)] = kv_part.astype(BF)
+        for n, c in enumerate(chunks):
+            cosine = cosines[c]
+            sine = sines[c]
+            for head in range(2):
+                v = q_part[n * CH : (n + 1) * CH, head * HD : (head + 1) * HD]
+                turned = v * cosine + pltpu.roll(v, HD // 2, 1) * sine
+                swapped = pltpu.roll(turned, HD // 2, 1)
+                first = jnp.where(low, turned, 0.0)
+                second = jnp.where(low, swapped, 0.0)
+                both_halves = jnp.concatenate([first, second], axis=1).astype(BF)
+                qpad[y, c, pl.ds(head * CH, CH), :] = both_halves
 
     def scores_of(queries, keys):
         return lax.dot_general(queries, keys, (((1,), (1,)), ((), ())), preferred_element_type=F32)
@@ -207,19 +208,21 @@
     def in_order(k):
         return (z + ((k + 1) // 2) * (2 * (k % 2) - 1) + NZ) % NZ
 
-    def project_own(first, last):
-        def body(k, carry):
-            project(in_order(k), lo)
-            return carry
-
-        lax.fori_loop(first, last, body, 0)
-
-    def project_other(first, last):
-        def body(k, carry):
-            c = in_order(k)
-            project(c, 1 - lo)
+    def send_kv(chunks):
+        for c in chunks:
             block = kv_rows(par, c)
             remote(block, block, KVZ + c, pair).start()
+
+    def around(h):
+        return ((z + h) % NZ, (z + NZ - h) % NZ)
+
+    def project_pairs(first, last, y, whole):
+        def body(h, carry):
+            chunks = around(h)
+            project_kv(chunks, y)
+            if whole:
+                send_kv(chunks)
+            project_q(chunks, y)
             return carry
 
         lax.fori_loop(first, last, body, 0)
@@ -252,8 +255,6 @@
         logical = logical + jnp.where(page_row == pages_ref[page], float(page), 0.0)
     key_pos = logical * 128.0 + lax.broadcasted_iota(jnp.int32, (32, 128), 1).astype(F32)
     kpe[...] = jnp.where(key_pos < SINKS, 1e6, key_pos)
-    project_own(0, 1)
-
     def kv_settle(c):
         arrived(kv_rows(1 - par, c), KVZ + c)
         left(kv_rows(par, c), KVZ + c)
@@ -293,14 +294,16 @@
         factor = jnp.exp2((state[0] - top) * SCALE)
         return (top, state[1] * factor + total, state[2] * factor + acc)
 
-    def offsets(c):
-        one = off[c]
-        return jnp.concatenate([one, one], axis=0)
-
-    def prefix_part(c):
-        offset = offsets(c)
+    def pair_queries(chunks, y):
+        return jnp.concatenate([qpad[y, c] for c in chunks], axis=0)
+
+    def pair_offsets(chunks):
+        return jnp.concatenate([off[c] for c in chunks for _ in range(2)], axis=0)
+
+    def prefix_part(chunks):
+        offset = pair_offsets(chunks)
         for y in range(2):
-            queries = qpad[y, c]
+            queries = pair_queries(chunks, y)
             state = None
             for b in range(4):
                 parts = []
@@ -310,18 +313,22 @@
                 keys = jnp.concatenate(parts, axis=0)
                 positions = jnp.concatenate([kpe[pl.ds(8 * b + r, 1), :] for r in range(8)], axis=1)
                 state = fold(state, queries, keys, positions > offset)
-            st_m[c, y] = state[0]
-            st_l[c, y] = state[1]
-            st_acc[c, y] = state[2]
-
-    def suffix_part(c, slot_out):
-        offset = offsets(c)
-        row = lax.broadcasted_iota(jnp.int32, (2 * CH, 1), 0) % CH + c * CH
-        row = row.astype(F32)
+            for n, c in enumerate(chunks):
+                st_m[c, y] = state[0][n * 2 * CH : (n + 1) * 2 * CH]
+                st_l[c, y] = state[1][n * 2 * CH : (n + 1) * 2 * CH]
+                st_acc[c, y] = state[2][n * 2 * CH : (n + 1) * 2 * CH]
+
+    def suffix_part(chunks):
+        offset = pair_offsets(chunks)
+        row = lax.broadcasted_iota(jnp.int32, (2 * CH, 1), 0) % CH
+        row = jnp.concatenate([row + c * CH for c in chunks], axis=0).astype(F32)
         column_index = lax.broadcasted_iota(jnp.int32, (1, HALF), 1).astype(F32)
+        lane2 = lax.broadcasted_iota(jnp.int32, (2 * CH * len(chunks), HD), 1)
         for y in range(2):
-            queries = qpad[y, c]
-            state = (st_m[c, y], st_l[c, y], st_acc[c, y])
+            queries = pair_queries(chunks, y)
+            state = tuple(
+                jnp.concatenate([ref[c, y] for c in chunks], axis=0) for ref in (st_m, st_l, st_acc)
+            )
             for slot in range(3):
                 keys = jnp.concatenate([kvs[slot, y, 0], kvs[slot, y, 1]], axis=1)
                 index = column_index + (slot - 2) * HALF
@@ -329,20 +336,23 @@
                 state = fold(state, queries, keys, visible)
             result = state[2] / state[1]
             first = pltpu.roll(result[:, :HD], HD // 2, 1)
-            lane2 = lax.broadcasted_iota(jnp.int32, (2 * CH, HD), 1)
             merged = jnp.where(lane2 < HD // 2, first, result[:, HD:]).astype(BF)
-            attn[slot_out, :, pl.ds(y * 256, HD)] = merged[:CH]
-            attn[slot_out, :, pl.ds(y * 256 + HD, HD)] = merged[CH:]
+            for n in range(len(chunks)):
+                for head in range(2):
+                    part = merged[(2 * n + head) * CH : (2 * n + head + 1) * CH]
+                    attn[pl.ds(n * CH, CH), pl.ds(y * 256 + head * HD, HD)] = part
 
     tile = 1024
 
-    def out_terms(slot):
+    def out_terms(second):
         @pl.loop(0, D // tile)
         def _(n):
             cols = pl.ds(pl.multiple_of(n * tile, tile), tile)
-            rows = attn[slot]
+            rows = attn[...]
             term = jnp.dot(rows[:, :256], wo[0, :, cols], preferred_element_type=F32)
-            tbuf[slot, :, cols] = term + jnp.dot(rows[:, 256:], wo[1, :, cols], preferred_element_type=F32)
+            term = term + jnp.dot(rows[:, 256:], wo[1, :, cols], preferred_element_type=F32)
+            tbuf[0, :, cols] = term[:CH]
+            tbuf[second, :, cols] = term[CH:]
 
     def rs_send(d, h, p):
         src = sbuf.at[d, h - 1, rows_of(p)]
@@ -352,48 +362,66 @@
     def rs_wait(d, h, p):
         arrived(rbuf.at[d, h - 1, rows_of(p)], ring_id(RS, d, h, p))
 
-    ring_step(1)
     arrived(px.at[1 - lo, hi, xx, core], PY)
     arrived(px.at[1 - lo, 1 - hi, xx, core], PY + 1)
     arrived(px.at[lo, 1 - hi, xx, core], PY + 2)
-    here = px.at[:, :, xx, core]
-    for k in range(1, 4):
-        remote(here, here, PX + k - 1, along_x(k)).start()
-    project_own(1, 3)
+
+    def x_block(k):
+        return px.at[:, :, (xx + k) % 4, core]
+
+    def x_half(k, which):
+        return px.at[:, :, (xx + k) % 4, core, which]
+
+    remote(x_block(0), x_block(0), PX, along_x(1)).start()
+    remote(x_block(0), x_block(0), PX + 1, along_x(3)).start()
+    local_wq.wait()
+    local_wkv.wait()
+    remote(wkv_half(lo), wkv_half(lo), WY + 1, weight_peer).start()
+    remote(wq_half(lo), wq_half(lo), WY, weight_peer).start()
+    project_kv((z,), lo)
+    project_q((z,), lo)
+    ring_step(1)
+    project_pairs(1, 2, lo, False)
+    arrived(x_block(3), PX)
+    remote(x_half(3, 0), x_half(3, 0), PX + 2, along_x(1)).start()
+    arrived(x_block(1), PX + 1)
+    remote(x_half(1, 1), x_half(1, 1), PX + 3, along_x(3)).start()
     ring_step(2)
+    arrived(wkv_half(1 - lo), WY + 1)
+    remote(wkv_half(1 - lo), wkv_half(1 - lo), WSIB + 1, sibling).start()
     arrived(wq_half(1 - lo), WY)
     remote(wq_half(1 - lo), wq_half(1 - lo), WSIB, sibling).start()
-    arrived(wkv_half(1 - lo), WY + 1)
-    remote(wkv_half(1 - lo), wkv_half(1 - lo), WSIB + 1, sibling).start()
     local_wo.wait()
     remote(wo_half(lo), wo_half(lo), WY + 2, weight_peer).start()
-    project_own(3, 5)
+    arrived(x_half(2, 0), PX + 2)
+    arrived(x_half(2, 1), PX + 3)
+    column = px.at[:, :, :, core]
+    remote(column, column, PSIB, sibling).start()
+    project_pairs(2, 3, lo, False)
     arrived(sib_rows(wq, D // 2), WSIB)
     arrived(sib_rows(wkv, 64), WSIB + 1)
-    project_other(0, 5)
+    project_kv((z,), 1 - lo)
+    send_kv((z,))
+    project_q((z,), 1 - lo)
+    project_pairs(1, 3, 1 - lo, True)
     ring_step(3)
-    for k in range(1, 4):
-        arrived(px.at[:, :, (xx + 4 - k) % 4, core], PX + k - 1)
-    column = px.at[:, :, :, core]
-    remote(column, column, PSIB, sibling).start()
-    project_own(5, 7)
-    project_other(5, 7)
+    project_pairs(3, 4, lo, False)
+    project_pairs(3, 4, 1 - lo, True)
     settle(0, 5)
+    arrived(px.at[:, :, :, 1 - core], PSIB)
     ring_wait(0, 4, 0)
     ring_wait(1, 4, 1)
-    project_own(7, 8)
-    project_other(7, 8)
+    far = (z + 4) % NZ
+    project_kv((far,), lo)
+    project_kv((far,), 1 - lo)
+    send_kv((far,))
+    project_q((far,), lo)
+    project_q((far,), 1 - lo)
+    settle(5, 8)
     arrived(wo_half(1 - lo), WY + 2)
     remote(wo_half(1 - lo), wo_half(1 - lo), WSIB + 2, sibling).start()
-    arrived(px.at[:, :, :, 1 - core], PSIB)
-
-    def early(k, carry):
-        prefix_part(in_order(k))
-        return carry
-
-    lax.fori_loop(7, 8, early, 0)
-    settle(5, 8)
-    lax.fori_loop(5, 7, early, 0)
+    prefix_part((far, z))
+    prefix_part(around(3))
 
     def kv_arrive(c, carry):
         for k in (1, 2):
@@ -404,8 +432,8 @@
     arrived(sib_rows(wo, 128), WSIB + 2)
 
     col_tiles = [pl.ds(n * tile, tile) for n in range(D // tile)]
-    suffix_part((z + 4) % NZ, 0)
-    out_terms(0)
+    suffix_part((far, z))
+    out_terms(2)
     for d in range(2):
         for cols in col_tiles:
             sbuf[d, 3, rows_of(d), cols] = tbuf[0, rows_of(d), cols].astype(BF)
@@ -414,18 +442,14 @@
     def reduce_step(i, carry):
         h = 3 - i
 
-        def terms(d, carry):
-            c = (z + (1 - 2 * d) * h + NZ) % NZ
-
-            @pl.when(i > 0)
-            def _():
-                prefix_part(c)
-
-            suffix_part(c, d)
-            out_terms(d)
-            return carry
-
-        lax.fori_loop(0, 2, terms, 0)
+        chunks = around(h)
+
+        @pl.when(i > 0)
+        def _():
+            prefix_part(chunks)
+
+        suffix_part(chunks)
+        out_terms(1)
         for fresh in (True, False):
             for d in range(2):
                 p = 1 - d if fresh else d
@@ -444,20 +468,19 @@
         return carry
 
     lax.fori_loop(0, 3, reduce_step, 0)
-    prefix_part(z)
-    suffix_part(z, 0)
-    out_terms(0)
     for p in range(2):
         for d in range(2):
             rs_wait(d, 1, p)
         for cols in col_tiles:
-            total = tbuf[0, rows_of(p), cols] + rbuf[0, 0, rows_of(p), cols].astype(F32)
+            total = tbuf[2, rows_of(p), cols] + rbuf[0, 0, rows_of(p), cols].astype(F32)
             out_ref[rows_of(p), cols] = (total + rbuf[1, 0, rows_of(p), cols].astype(F32)).astype(BF)
 
     left(mine, PZ)
     for k in range(3):
         left(both, PY + k)
-        left(here, PX + k)
+    for k in range(2):
+        left(x_block(0), PX + k)
+        left(x_half(3 - 2 * k, k), PX + 2 + k)
     left(column, PSIB)
     for k, half in enumerate((wq_half, wkv_half, wo_half)):
         left(half(lo), WY + k)
@@ -498,12 +521,12 @@
             pltpu.VMEM((NZ, 2, 2 * CH, 1), F32),
             pltpu.VMEM((NZ, 2, 2 * CH, 1), F32),
             pltpu.VMEM((NZ, 2, 2 * CH, 256), F32),
-            pltpu.VMEM((2, CH, 512), BF),
+            pltpu.VMEM((2 * CH, 512), BF),
             pltpu.VMEM((32, 128), F32),
             pltpu.VMEM((NZ, CH, 1), F32),
             pltpu.VMEM((NZ, CH, HD), F32),
             pltpu.VMEM((NZ, CH, HD), F32),
-            pltpu.VMEM((2, CH, D), F32),
+            pltpu.VMEM((3, CH, D), F32),
             pltpu.VMEM((2, 4, CH, D), BF),
             pltpu.VMEM((2, 4, CH, D), BF),
             pltpu.SemaphoreType.DMA((MESSAGES,)),
@@ -511,7 +534,7 @@
             pltpu.SemaphoreType.DMA((3,)),
         ],
         compiler_params=pltpu.CompilerParams(
-            collective_id=0, has_side_effects=True, vmem_limit_bytes=60 << 20
+            collective_id=0, has_side_effects=True, vmem_limit_bytes=63 << 20
         ),
     )(
         x_rows,

time: 136 us -> 118 us (0.87)
  Pallas kernels: 133 us -> 115 us
    pallas_call x1, Pallas kernels: 133 us -> 115 us  [local(): pl.pallas_call(kernel, out_shape=jax.ShapeDtypeStruct((CH, D), BF), in_sp...]
where the time goes in v3:
time: 118 us; the launch traced here: 117 us
  Pallas kernels  115 us (97%)
  local copies, waits for them, and re-layouts  1.87 us (2%)
    pallas_call x1, Pallas kernels, local(): pl.pallas_call(kernel, out_shape=jax.ShapeDtypeStruct((CH, D), BF), in_sp...  115 us

profile of v3, /device:TPU:1, one launch (start us, length us, event | category | flops | bytes accessed | tf_op | source)
XLA Modules:
  0.0 116.8 jit_solution(10723698996128045401)
XLA Ops:
  0.0 114.9 %shard_map.91 = bf16[64,4096]{1,0:T(8,128)(2,1)} custom-call(bf16[64,4096]{1,0:T(8,128)(2,1)} %x_ref.1, f32[1,4096]{1,0:T(1,128)} %bitcast.11, bf16[256,128]{1,0:T(8,128)(2,1)} %bitcast.9, s32[128,128]{1,0:T(8,128)} %bitcast.10, f32[1,128]{1,0:T(1,128)} %constant.5.freq_ref, s32[32]{0:T(128)} %pages_ref.1, bf16[4096,256]{1,0:T(8,128)(2,1)} %wq_ref.1, ...), custom_call_target="tpu_custom_call" | custom-call | tf_op jit(solution)/shard_map/pallas_call | solution.py:508
  114.9 1.9 %copy.11 = bf16[64,4096]{1,0:T(8,128)(2,1)} copy(bf16[64,4096]{1,0:T(8,128)(2,1)} %shard_map.91) | data formatting | bytes 1048576

commit v4 on v3

--- a/solution.py
+++ b/solution.py
@@ -21,8 +21,9 @@
 BF = jnp.bfloat16
 F32 = jnp.float32
 
-RING, PZ, PY, PX, PSIB, WY, WSIB, KVZ, KVH, RS = 0, 16, 17, 20, 24, 25, 28, 31, 39, 55
-MESSAGES = 71
+RING, PZ, PY, PX, PSIB, WY, WSIB = 0, 16, 17, 20, 24, 25, 28
+VZ, VY, VX, VSIB, KVH, RS = 31, 32, 35, 39, 40, 56
+MESSAGES = 72
 
 
 def ring_id(base, d, h, p):
@@ -43,6 +44,7 @@
     xall,
     wq,
     wkv,
+    wv,
     wo,
     px,
     kvs,
@@ -110,6 +112,13 @@
     def origin(d, h):
         return (z - sign[d] * h + NZ) % NZ
 
+    partners = [up, down, (g, other_t), (other_g, other_t), (other_g, t)]
+    partners += [along_x(1), along_x(3), sibling]
+    partners += [half_group(1), half_group(-1), half_group(2), half_group(-2)]
+    barrier = pltpu.get_barrier_semaphore()
+    for device in partners:
+        pl.semaphore_signal(barrier, inc=1, device_id=device, device_id_type=MESH)
+
     local_wq = pltpu.make_async_copy(wq_ref, wq.at[lo], lsem.at[0])
     local_wkv = pltpu.make_async_copy(wkv_ref, wkv.at[lo], lsem.at[1])
     local_wo = pltpu.make_async_copy(wo_ref, wo.at[lo], lsem.at[2])
@@ -125,14 +134,12 @@
     for d in range(2):
         rbuf[d, 3, rows_of(1 - d)] = jnp.zeros((32, D), BF)
 
-    partners = [up, down, (g, other_t), (other_g, other_t), (other_g, t)]
-    partners += [along_x(1), along_x(3), sibling]
-    partners += [half_group(1), half_group(-1), half_group(2), half_group(-2)]
-    barrier = pltpu.get_barrier_semaphore()
-    for device in partners:
-        pl.semaphore_signal(barrier, inc=1, device_id=device, device_id_type=MESH)
     pl.semaphore_wait(barrier, len(partners))
 
+    local_wkv.wait()
+    slice_of_mine = wkv.at[lo, :, pl.ds(pl.multiple_of(g * 256, 256), 256)]
+    slice_of_pair = wv.at[lo, hi, xx, core]
+    remote(slice_of_mine, slice_of_pair, VZ, pair).start()
     mine = px.at[lo, hi, xx, core, par]
     remote(mine, mine, PZ, pair).start()
 
@@ -159,30 +166,34 @@
     def sib_rows(ref, size):
         return ref.at[1 - lo, pl.ds(pl.multiple_of((1 - core) * size, size), size)]
 
-    arrived(px.at[lo, hi, xx, core, 1 - par], PZ)
-    both = px.at[lo, hi, xx, core]
-    remote(both, both, PY, (g, other_t)).start()
-    remote(both, both, PY + 1, (other_g, other_t)).start()
-    remote(both, both, PY + 2, (other_g, t)).start()
-
-    def ring_step(h):
-        for p in range(2):
-            for d in range(2):
-                if h < 3 or p == d:
-                    ring_wait(d, h, p)
-                    ring_send(d, h + 1, p)
-        if h == 3:
-            for d in range(2):
-                ring_wait(d, h, 1 - d)
+    def ring_pass(h, p):
+        for d in range(2):
+            ring_wait(d, h, p)
+            if h < 3 or p == d:
+                ring_send(d, h + 1, p)
 
     lane = lax.broadcasted_iota(jnp.int32, (CH, HD), 1)
     low = lane < HD // 2
 
-    def project_kv(chunks, y):
+    def project_kv(chunks):
         rows = jnp.concatenate([xall[c] for c in chunks], axis=0)
-        kv_part = scores_of(rows, wkv[y]).astype(BF)
+        own = scores_of(rows, jnp.concatenate([wkv[0], wkv[1]], axis=0)).astype(BF).astype(F32)
+        other = None
+        for k in range(16):
+            at = (k // 8, (k // 2) % 4, k % 2)
+            weights = jnp.concatenate([wv[(0,) + at], wv[(1,) + at]], axis=0)
+            part = scores_of(rows[:, k * 256 : (k + 1) * 256], weights)
+            other = part if other is None else other + part
+        other = other.astype(BF).astype(F32)
         for n, c in enumerate(chunks):
-            kvs[2, y, par, pl.ds(pl.multiple_of(c * CH, CH), CH)] = kv_part[n * CH : (n + 1) * CH]
+            cosine = jnp.where(low, cosines[c], 1.0)
+            sine = jnp.where(low, -sines[c], 0.0) * turn
+            rows_here = pl.ds(pl.multiple_of(c * CH, CH), CH)
+            for y in range(2):
+                first = own[n * CH : (n + 1) * CH, y * HD : (y + 1) * HD]
+                second = other[n * CH : (n + 1) * CH, y * HD : (y + 1) * HD]
+                kvs[2, y, par, rows_here] = (first * cosine - second * sine).astype(BF)
+                kvs[2, y, 1 - par, rows_here] = (second * cosine + first * sine).astype(BF)
 
     def project_q(chunks, y):
         rows = jnp.concatenate([xall[c] for c in chunks], axis=0)
@@ -202,30 +213,19 @@
     def scores_of(queries, keys):
         return lax.dot_general(queries, keys, (((1,), (1,)), ((), ())), preferred_element_type=F32)
 
-    def kv_rows(which, c):
-        return kvs.at[2, :, which, pl.ds(pl.multiple_of(c * CH, CH), CH)]
-
-    def in_order(k):
-        return (z + ((k + 1) // 2) * (2 * (k % 2) - 1) + NZ) % NZ
-
-    def send_kv(chunks):
-        for c in chunks:
-            block = kv_rows(par, c)
-            remote(block, block, KVZ + c, pair).start()
+    turn = (1 - 2 * par).astype(F32)
+
+    def kv_chunk(slot, c):
+        return kvs.at[slot, :, :, pl.ds(pl.multiple_of(c * CH, CH), CH)]
 
     def around(h):
         return ((z + h) % NZ, (z + NZ - h) % NZ)
 
-    def project_pairs(first, last, y, whole):
-        def body(h, carry):
-            chunks = around(h)
-            project_kv(chunks, y)
-            if whole:
-                send_kv(chunks)
-            project_q(chunks, y)
-            return carry
-
-        lax.fori_loop(first, last, body, 0)
+    def project_whole_kv(chunks):
+        project_kv(chunks)
+        for c in chunks:
+            for k in (1, 2):
+                remote(kv_chunk(2, c), kv_chunk(2 - k, c), KVH + 2 * c + k - 1, half_group(k)).start()
 
     pieces = []
     for k in range(3):
@@ -248,37 +248,12 @@
         sines[c] = jnp.where(low, -sine, sine)
         return carry
 
-    lax.fori_loop(0, NZ, tables, 0)
     page_row = lax.broadcasted_iota(jnp.int32, (32, 128), 0)
     logical = jnp.zeros((32, 128), F32)
     for page in range(32):
         logical = logical + jnp.where(page_row == pages_ref[page], float(page), 0.0)
     key_pos = logical * 128.0 + lax.broadcasted_iota(jnp.int32, (32, 128), 1).astype(F32)
     kpe[...] = jnp.where(key_pos < SINKS, 1e6, key_pos)
-    def kv_settle(c):
-        arrived(kv_rows(1 - par, c), KVZ + c)
-        left(kv_rows(par, c), KVZ + c)
-        rows = pl.ds(pl.multiple_of(c * CH, CH), CH)
-        cosine = jnp.where(low, cosines[c], 1.0)
-        sine = jnp.where(low, -sines[c], 0.0)
-        for y in range(2):
-            first = kvs[2, y, 0, rows].astype(F32)
-            second = kvs[2, y, 1, rows].astype(F32)
-            kvs[2, y, 0, rows] = (first * cosine - second * sine).astype(BF)
-            kvs[2, y, 1, rows] = (second * cosine + first * sine).astype(BF)
-        for k in (1, 2):
-            remote(kv_chunk(2, c), kv_chunk(2 - k, c), KVH + 2 * c + k - 1, half_group(k)).start()
-
-    def kv_chunk(slot, c):
-        return kvs.at[slot, :, :, pl.ds(pl.multiple_of(c * CH, CH), CH)]
-
-    def settle(first, last):
-        def body(k, carry):
-            kv_settle(in_order(k))
-            return carry
-
-        lax.fori_loop(first, last, body, 0)
-
     def fold(state, queries, keys, visible):
         scores = jnp.where(visible, scores_of(queries, keys), NEG)
         highest = jnp.max(scores, axis=-1, keepdims=True)
@@ -305,13 +280,13 @@
         for y in range(2):
             queries = pair_queries(chunks, y)
             state = None
-            for b in range(4):
+            for b in range(8):
                 parts = []
-                for k in range(4):
-                    at = (y, b // 2, (b % 2) * 2 + k // 2, k % 2)
+                for k in range(2):
+                    at = (y, b // 4, b % 4, k)
                     parts.append(jnp.concatenate([px[at + (0,)], px[at + (1,)]], axis=1))
                 keys = jnp.concatenate(parts, axis=0)
-                positions = jnp.concatenate([kpe[pl.ds(8 * b + r, 1), :] for r in range(8)], axis=1)
+                positions = jnp.concatenate([kpe[pl.ds(4 * b + r, 1), :] for r in range(4)], axis=1)
                 state = fold(state, queries, keys, positions > offset)
             for n, c in enumerate(chunks):
                 st_m[c, y] = state[0][n * 2 * CH : (n + 1) * 2 * CH]
@@ -362,67 +337,93 @@
     def rs_wait(d, h, p):
         arrived(rbuf.at[d, h - 1, rows_of(p)], ring_id(RS, d, h, p))
 
-    arrived(px.at[1 - lo, hi, xx, core], PY)
-    arrived(px.at[1 - lo, 1 - hi, xx, core], PY + 1)
-    arrived(px.at[lo, 1 - hi, xx, core], PY + 2)
-
     def x_block(k):
         return px.at[:, :, (xx + k) % 4, core]
 
     def x_half(k, which):
         return px.at[:, :, (xx + k) % 4, core, which]
 
+    y_side = ((g, other_t), (other_g, other_t), (other_g, t))
+    arrived(slice_of_pair, VZ)
+    for k in range(3):
+        remote(slice_of_pair, slice_of_pair, VY + k, y_side[k]).start()
+    arrived(px.at[lo, hi, xx, core, 1 - par], PZ)
+    both = px.at[lo, hi, xx, core]
+    for k in range(3):
+        remote(both, both, PY + k, y_side[k]).start()
+    remote(wkv_half(lo), wkv_half(lo), WY + 1, weight_peer).start()
+    local_wq.wait()
+    remote(wq_half(lo), wq_half(lo), WY, weight_peer).start()
+    from_y = ((1 - lo, hi), (1 - lo, 1 - hi), (lo, 1 - hi))
+    for k in range(3):
+        arrived(wv.at[from_y[k][0], from_y[k][1], xx, core], VY + k)
+
+    def v_block(k):
+        return wv.at[:, :, (xx + k) % 4, core]
+
+    def v_half(k, which):
+        return wv.at[which, :, (xx + k) % 4, core]
+
+    remote(v_block(0), v_block(0), VX, along_x(1)).start()
+    remote(v_block(0), v_block(0), VX + 1, along_x(3)).start()
+    lax.fori_loop(0, NZ, tables, 0)
+    for k in range(3):
+        arrived(px.at[from_y[k][0], from_y[k][1], xx, core], PY + k)
+    project_q((z,), lo)
+    ring_pass(1, 0)
+    arrived(v_block(3), VX)
+    remote(v_half(3, 0), v_half(3, 0), VX + 2, along_x(1)).start()
+    arrived(v_block(1), VX + 1)
+    remote(v_half(1, 1), v_half(1, 1), VX + 3, along_x(3)).start()
     remote(x_block(0), x_block(0), PX, along_x(1)).start()
     remote(x_block(0), x_block(0), PX + 1, along_x(3)).start()
-    local_wq.wait()
-    local_wkv.wait()
-    remote(wkv_half(lo), wkv_half(lo), WY + 1, weight_peer).start()
-    remote(wq_half(lo), wq_half(lo), WY, weight_peer).start()
-    project_kv((z,), lo)
-    project_q((z,), lo)
-    ring_step(1)
-    project_pairs(1, 2, lo, False)
+    ring_pass(1, 1)
+    arrived(v_half(2, 0), VX + 2)
+    arrived(v_half(2, 1), VX + 3)
+    v_column = wv.at[:, :, :, core]
+    remote(v_column, v_column, VSIB, sibling).start()
+    arrived(wkv_half(1 - lo), WY + 1)
+    remote(wkv_half(1 - lo), wkv_half(1 - lo), WSIB + 1, sibling).start()
+    project_q(around(1), lo)
+    ring_pass(2, 0)
+    arrived(wv.at[:, :, :, 1 - core], VSIB)
+    arrived(sib_rows(wkv, 64), WSIB + 1)
+    project_whole_kv((z,))
+    project_whole_kv(around(1))
+    ring_pass(2, 1)
     arrived(x_block(3), PX)
     remote(x_half(3, 0), x_half(3, 0), PX + 2, along_x(1)).start()
     arrived(x_block(1), PX + 1)
     remote(x_half(1, 1), x_half(1, 1), PX + 3, along_x(3)).start()
-    ring_step(2)
-    arrived(wkv_half(1 - lo), WY + 1)
-    remote(wkv_half(1 - lo), wkv_half(1 - lo), WSIB + 1, sibling).start()
     arrived(wq_half(1 - lo), WY)
     remote(wq_half(1 - lo), wq_half(1 - lo), WSIB, sibling).start()
+    project_whole_kv(around(2))
+    ring_pass(3, 0)
     local_wo.wait()
     remote(wo_half(lo), wo_half(lo), WY + 2, weight_peer).start()
+    project_q(around(2), lo)
+    arrived(sib_rows(wq, D // 2), WSIB)
+    project_q((z,), 1 - lo)
+    project_q(around(1), 1 - lo)
     arrived(x_half(2, 0), PX + 2)
     arrived(x_half(2, 1), PX + 3)
     column = px.at[:, :, :, core]
     remote(column, column, PSIB, sibling).start()
-    project_pairs(2, 3, lo, False)
-    arrived(sib_rows(wq, D // 2), WSIB)
-    arrived(sib_rows(wkv, 64), WSIB + 1)
-    project_kv((z,), 1 - lo)
-    send_kv((z,))
-    project_q((z,), 1 - lo)
-    project_pairs(1, 3, 1 - lo, True)
-    ring_step(3)
-    project_pairs(3, 4, lo, False)
-    project_pairs(3, 4, 1 - lo, True)
-    settle(0, 5)
+    ring_pass(3, 1)
+    project_whole_kv(around(3))
+    project_q(around(3), lo)
+    project_q(around(3), 1 - lo)
     arrived(px.at[:, :, :, 1 - core], PSIB)
+    prefix_part(around(3))
     ring_wait(0, 4, 0)
     ring_wait(1, 4, 1)
     far = (z + 4) % NZ
-    project_kv((far,), lo)
-    project_kv((far,), 1 - lo)
-    send_kv((far,))
+    project_whole_kv((far,))
     project_q((far,), lo)
     project_q((far,), 1 - lo)
-    settle(5, 8)
+    prefix_part((far, z))
     arrived(wo_half(1 - lo), WY + 2)
     remote(wo_half(1 - lo), wo_half(1 - lo), WSIB + 2, sibling).start()
-    prefix_part((far, z))
-    prefix_part(around(3))
-
     def kv_arrive(c, carry):
         for k in (1, 2):
             arrived(kv_chunk(2 - k, c), KVH + 2 * c + k - 1)
@@ -438,6 +439,7 @@
         for cols in col_tiles:
             sbuf[d, 3, rows_of(d), cols] = tbuf[0, rows_of(d), cols].astype(BF)
         rs_send(d, 4, d)
+    project_q(around(2), 1 - lo)
 
     def reduce_step(i, carry):
         h = 3 - i
@@ -478,10 +480,15 @@
     left(mine, PZ)
     for k in range(3):
         left(both, PY + k)
+        left(slice_of_pair, VY + k)
     for k in range(2):
         left(x_block(0), PX + k)
         left(x_half(3 - 2 * k, k), PX + 2 + k)
+        left(v_block(0), VX + k)
+        left(v_half(3 - 2 * k, k), VX + 2 + k)
     left(column, PSIB)
+    left(slice_of_mine, VZ)
+    left(v_column, VSIB)
     for k, half in enumerate((wq_half, wkv_half, wo_half)):
         left(half(lo), WY + k)
         left(half(1 - lo), WSIB + k)
@@ -514,6 +521,7 @@
             pltpu.VMEM((NZ, CH, D), BF),
             pltpu.VMEM((2, D, 256), BF),
             pltpu.VMEM((2, 128, D), BF),
+            pltpu.VMEM((2, 2, 4, 2, 128, 256), BF),
             pltpu.VMEM((2, 256, D), BF),
             pltpu.VMEM((2, 2, 4, 2, 2, 256, 128), BF),
             pltpu.VMEM((3, 2, 2, HALF, 128), BF),

time: 118 us -> 118 us (level)
  no operation moved by 1% of the time
where the time goes in v4:
time: 118 us; the launch traced here: 117 us
  Pallas kernels  116 us (98%)
  local copies, waits for them, and re-layouts  1.87 us (2%)
    pallas_call x1, Pallas kernels, local(): pl.pallas_call(kernel, out_shape=jax.ShapeDtypeStruct((CH, D), BF), in_sp...  116 us

profile of v4, /device:TPU:1, one launch (start us, length us, event | category | flops | bytes accessed | tf_op | source)
XLA Modules:
  0.0 117.5 jit_solution(8121450253470312271)
XLA Ops:
  0.0 115.6 %shard_map.91 = bf16[64,4096]{1,0:T(8,128)(2,1)} custom-call(bf16[64,4096]{1,0:T(8,128)(2,1)} %x_ref.1, f32[1,4096]{1,0:T(1,128)} %bitcast.11, bf16[256,128]{1,0:T(8,128)(2,1)} %bitcast.9, s32[128,128]{1,0:T(8,128)} %bitcast.10, f32[1,128]{1,0:T(1,128)} %constant.5.freq_ref, s32[32]{0:T(128)} %pages_ref.1, bf16[4096,256]{1,0:T(8,128)(2,1)} %wq_ref.1, ...), custom_call_target="tpu_custom_call" | custom-call | tf_op jit(solution)/shard_map/pallas_call | solution.py:515
  115.6 1.9 %copy.11 = bf16[64,4096]{1,0:T(8,128)(2,1)} copy(bf16[64,4096]{1,0:T(8,128)(2,1)} %shard_map.91) | data formatting | bytes 1048576

commit v5 on v4

--- a/solution.py
+++ b/solution.py
@@ -275,9 +275,9 @@
     def pair_offsets(chunks):
         return jnp.concatenate([off[c] for c in chunks for _ in range(2)], axis=0)
 
-    def prefix_part(chunks):
+    def prefix_part(chunks, heads=(0, 1)):
         offset = pair_offsets(chunks)
-        for y in range(2):
+        for y in heads:
             queries = pair_queries(chunks, y)
             state = None
             for b in range(8):
@@ -421,19 +421,20 @@
     project_whole_kv((far,))
     project_q((far,), lo)
     project_q((far,), 1 - lo)
-    prefix_part((far, z))
+    prefix_part((far, z), (0,))
     arrived(wo_half(1 - lo), WY + 2)
     remote(wo_half(1 - lo), wo_half(1 - lo), WSIB + 2, sibling).start()
+    prefix_part((far, z), (1,))
     def kv_arrive(c, carry):
         for k in (1, 2):
             arrived(kv_chunk(2 - k, c), KVH + 2 * c + k - 1)
         return carry
 
     lax.fori_loop(0, NZ, kv_arrive, 0)
-    arrived(sib_rows(wo, 128), WSIB + 2)
 
     col_tiles = [pl.ds(n * tile, tile) for n in range(D // tile)]
     suffix_part((far, z))
+    arrived(sib_rows(wo, 128), WSIB + 2)
     out_terms(2)
     for d in range(2):
         for cols in col_tiles:

time: 118 us -> 116 us (0.983)
  Pallas kernels: 116 us -> 114 us
    pallas_call x1, Pallas kernels: 116 us -> 114 us  [local(): pl.pallas_call(kernel, out_shape=jax.ShapeDtypeStruct((CH, D), BF), in_sp...]
where the time goes in v5:
time: 116 us
  Pallas kernels  114 us (98%)
  local copies, waits for them, and re-layouts  1.87 us (2%)
    pallas_call x1, Pallas kernels, local(): pl.pallas_call(kernel, out_shape=jax.ShapeDtypeStruct((CH, D), BF), in_sp...  114 us

profile of v5, /device:TPU:1, one launch (start us, length us, event | category | flops | bytes accessed | tf_op | source)
XLA Modules:
  0.0 115.9 jit_solution(92292721791976495)
XLA Ops:
  0.0 114.0 %shard_map.91 = bf16[64,4096]{1,0:T(8,128)(2,1)} custom-call(bf16[64,4096]{1,0:T(8,128)(2,1)} %x_ref.1, f32[1,4096]{1,0:T(1,128)} %bitcast.11, bf16[256,128]{1,0:T(8,128)(2,1)} %bitcast.9, s32[128,128]{1,0:T(8,128)} %bitcast.10, f32[1,128]{1,0:T(1,128)} %constant.5.freq_ref, s32[32]{0:T(128)} %pages_ref.1, bf16[4096,256]{1,0:T(8,128)(2,1)} %wq_ref.1, ...), custom_call_target="tpu_custom_call" | custom-call | tf_op jit(solution)/shard_map/pallas_call | solution.py:516
  114.0 1.9 %copy.11 = bf16[64,4096]{1,0:T(8,128)(2,1)} copy(bf16[64,4096]{1,0:T(8,128)(2,1)} %shard_map.91) | data formatting | bytes 1048576
